TPU v7x, 256 devices: a whole 4x4x8 slice. The times are simulated.
256 devices in a mesh: group: 32 (over x, z), span: 8 (over y, core).
Axes of the slice: x: 4, y: 4, z: 8, core: 2. Of those that a mesh axis runs over, the one named last changes fastest.
Arguments:
- struct_disp: float32 [3, 524288], P(None, ('group', 'span')), may hold values from -6 to 6
- interp_weight: float32 [524288, 4], P(('group', 'span')), may hold values from 0.2 to 1
- face_owner: int32 [524288, 4], P(('group', 'span')), may hold values from 0 to 31, all different within a row; in each aligned block of 2048 rows (0 to 2047, 2048 to 4095, ...) at most 512 rows name the same one
- face_row: int32 [524288, 4], P(('group', 'span')), may hold values from 0 to 20479
- skel_force: float32 [3, 16384], P(None, ('group', 'span')), may hold values from -6 to 6
- skel_coupling: float32 [6, 16384], P(None, ('group', 'span')), may hold values from 0.1 to 0.2
- skel_stiff: float32 [16384], P(('group', 'span')), may hold values from 0.05 to 0.15
- skel_edges: int32 [6, 16384], P(None, ('group', 'span')), may hold values from 0 to 16383
- block_spacing: float32 [3, 256], P(None, 'group'), may hold values from 1 to 2
Outputs:
- displacement: float32 [3, 256, 64, 6400], P(None, 'group', 'span')
- jacobian: float32 [256, 64, 6400], P('group', 'span')
Inputs may be any that keep to these rules, and one draw needn't show every extreme that they name: `face_owner`: each row names 4 different group indices; among the rows of one device no index is named more than 512 times, a bound that some block reaches.
All inputs are finite; a program needn't handle non-finite values.
Results may differ from a plain program's by a relative error of at most 0.0001.
Values sent between devices are 32-bit elements; how exact they have to be, the bound alone decides.
A program may use at most 128 MiB of HBM per device.

v0:
```python
import jax
import jax.numpy as jnp
from jax import lax
from jax.sharding import PartitionSpec as P

BPD = 8
SPAN_DEV = 8
NP = 80
ITERS = 4


def with_halo(block, sides, width):
    for axis, dim in sides:
        count = lax.axis_size(axis)
        forward = [(i, i + 1) for i in range(count - 1)]
        backward = [(target, source) for source, target in forward]
        low = lax.ppermute(
            lax.slice_in_dim(block, block.shape[dim] - width, None, axis=dim), axis, forward
        )
        high = lax.ppermute(lax.slice_in_dim(block, 0, width, axis=dim), axis, backward)
        block = jnp.concatenate([low, block, high], axis=dim)
    return block


def tfi_tables(points):
    position = jnp.arange(points * points, dtype=jnp.int32)
    first = position % points
    second = position // points
    frac_first = first.astype(jnp.float32) / (points - 1)
    frac_second = second.astype(jnp.float32) / (points - 1)
    edge_pos = jnp.arange(points, dtype=jnp.int32)[:, None]
    zero = jnp.zeros((points, points * points), jnp.float32)
    bottom = jnp.where(first[None] == edge_pos, (1.0 - frac_second)[None], zero)
    bottom = bottom.at[0].add(-(1.0 - frac_first) * (1.0 - frac_second))
    bottom = bottom.at[points - 1].add(-frac_first * (1.0 - frac_second))
    top_rows = jnp.where(first[None] == edge_pos, frac_second[None], zero)
    top_rows = top_rows.at[0].add(-(1.0 - frac_first) * frac_second)
    top_rows = top_rows.at[points - 1].add(-frac_first * frac_second)
    left_rows = jnp.where(second[None] == edge_pos, (1.0 - frac_first)[None], zero)
    right_rows = jnp.where(second[None] == edge_pos, frac_first[None], zero)
    table = jnp.concatenate([bottom, top_rows, left_rows, right_rows], axis=0)
    bubble = 16.0 * frac_first * (1.0 - frac_first) * frac_second * (1.0 - frac_second)
    return (table, bubble)


def plane_derivs(field, points):
    position = jnp.arange(points * points, dtype=jnp.int32)
    first = position % points
    second = position // points
    ahead = jnp.concatenate([field[..., 1:], field[..., -1:]], axis=-1)
    behind = jnp.concatenate([field[..., :1], field[..., :-1]], axis=-1)
    deriv_first = (
        jnp.where(first == points - 1, field, ahead) - jnp.where(first == 0, field, behind)
    ) * 0.5
    upper = jnp.concatenate([field[..., points:], field[..., -points:]], axis=-1)
    lower = jnp.concatenate([field[..., :points], field[..., :-points]], axis=-1)
    deriv_second = (
        jnp.where(second == points - 1, field, upper) - jnp.where(second == 0, field, lower)
    ) * 0.5
    return (deriv_first, deriv_second)


def metric_det(spacing, deriv_first, deriv_second, deriv_span):
    derivs = (deriv_first, deriv_second, deriv_span)
    matrix = [[derivs[col][row] for col in range(3)] for row in range(3)]
    for row in range(3):
        matrix[row][row] = matrix[row][row] + spacing[row][:, None, None]
    minor_one = matrix[1][1] * matrix[2][2] - matrix[1][2] * matrix[2][1]
    minor_two = matrix[1][0] * matrix[2][2] - matrix[1][2] * matrix[2][0]
    minor_three = matrix[1][0] * matrix[2][1] - matrix[1][1] * matrix[2][0]
    return matrix[0][0] * minor_one - matrix[0][1] * minor_two + matrix[0][2] * minor_three


def blend_layers(faces, skel_values, table, bubble):
    blended = jnp.dot(
        faces.reshape(-1, faces.shape[-1]),
        table,
        precision=lax.Precision.HIGHEST,
        preferred_element_type=jnp.float32,
    )
    shape = faces.shape[:-1] + (bubble.shape[0],)
    return blended.reshape(shape) + skel_values * bubble


def on_device(
    struct_disp,
    interp_weight,
    face_owner,
    face_row,
    skel_force,
    skel_coupling,
    skel_stiff,
    skel_edges,
    block_spacing,
):
    group_count = lax.axis_size("group")
    local_nodes = skel_force.shape[1]
    face_total = BPD * SPAN_DEV * 4 * NP
    weighted = (struct_disp[:, :, None] * interp_weight[None]).reshape(3, -1)
    owners = face_owner.reshape(-1)
    targets = face_row.reshape(-1)
    empty_faces = jnp.zeros((3, face_total), jnp.float32)
    contributions = owners.shape[0]
    capacity = 2 * contributions // group_count
    one_hot = (owners[:, None] == jnp.arange(group_count, dtype=jnp.int32)[None]).astype(jnp.int32)
    running = jnp.cumsum(one_hot, axis=0)
    slot_index = jnp.sum((running - 1) * one_hot, axis=1)
    send_values = (
        jnp.zeros((group_count, 3, capacity), jnp.float32).at[owners, :, slot_index].set(weighted.T)
    )
    send_rows = jnp.zeros((group_count, capacity), jnp.int32).at[owners, slot_index].set(targets)
    recv_values, recv_rows = (
        lax.all_to_all(send_values, "group", split_axis=0, concat_axis=0, tiled=True),
        lax.all_to_all(send_rows, "group", split_axis=0, concat_axis=0, tiled=True),
    )
    face_disp = empty_faces.at[:, recv_rows.reshape(-1)].add(
        recv_values.transpose(1, 0, 2).reshape(3, -1)
    )
    face_disp = face_disp.reshape(3, BPD, SPAN_DEV, 4 * NP)
    skeleton_rhs = skel_force + (0.25 * jnp.sum(face_disp, axis=3)).reshape(3, local_nodes)
    diagonal = skel_stiff + jnp.sum(skel_coupling, axis=0)

    def sweep(sweep_index, state):
        whole_state = lax.all_gather(state, ("group", "span"), axis=1, tiled=True)
        neighbours = whole_state[:, skel_edges]
        return (skeleton_rhs + jnp.sum(skel_coupling[None] * neighbours, axis=1)) / diagonal

    skeleton = lax.fori_loop(0, ITERS, sweep, jnp.zeros((3, local_nodes), jnp.float32))
    table, bubble = tfi_tables(NP)
    skel_layers = skeleton.reshape(3, BPD, SPAN_DEV, 1)
    displacement = blend_layers(face_disp, skel_layers, table, bubble)
    deriv_first, deriv_second = plane_derivs(displacement, NP)
    padded = with_halo(displacement, (("span", 2),), 1)
    deriv_span = (padded[:, :, 2:] - padded[:, :, :-2]) * 0.5
    jacobian = metric_det(block_spacing, deriv_first, deriv_second, deriv_span)
    return (displacement, jacobian)


def solution(mesh):
    return jax.shard_map(
        on_device,
        mesh=mesh,
        in_specs=(
            P(None, ("group", "span")),
            P(("group", "span"), None),
            P(("group", "span"), None),
            P(("group", "span"), None),
            P(None, ("group", "span")),
            P(None, ("group", "span")),
            P(("group", "span")),
            P(None, ("group", "span")),
            P(None, "group"),
        ),
        out_specs=(P(None, "group", "span", None), P("group", "span", None)),
        check_vma=False,
    )
```

profile of v0, /device:TPU:1, one launch (start us, length us, event | category | flops | bytes accessed | tf_op | source)
XLA Modules:
  0.0 606.8 jit_solution(6317149871625907783)
XLA Ops:
  0.6 1.1 copy.36
  1.8 0.6 eq.108
  2.4 0.6 eq.104
  3.1 0.7 reshape.355
  3.9 9.5 %reduce-window.6 = s32[32,64,128]{2,1,0:T(8,128)S(1)} reduce-window(s32[32,64,128]{2,1,0:T(8,128)S(1)} %fusion.34, s32[]{:T(128)} %constant.154.clone.1), window={size=1x1x128 pad=0_0x0_0x127_0}, to_apply=%region_0.0 | reduce-window | flops 33292288 | bytes 2097156 | tf_op jit(solution)/shard_map/reduce-window
  13.5 0.9 slice_reduce_fusion
  15.0 0.8 fusion.33
  16.6 0.6 reshape.387
  17.2 31.0 %scatter_custom_fusion.1 = s32[16384]{0:T(1024)} fusion(s32[8192]{0:T(1024)S(1)} %broadcast_select_fusion, s32[8192]{0:T(1024)S(1)} %reshape.387, s32[]{:T(128)} %constant.154.clone.1), kind=kCustom, calls=%fused_computation.84 | custom fusion | bytes 65540
  48.2 11.9 %all-to-all-start = ((s32[32,1,512]{2,1,0:T(1,128)}), s32[32,1,512]{2,1,0:T(1,128)S(1)}, u32[]{:S(2)}, u32[]{:S(2)}) async-start(s32[32,1,512]{2,1,0:T(1,128)} %bitcast.2), calls=%async_computation | async-start | bytes 131072 | tf_op jit(solution)/shard_map/all_to_all | solution.py:114
  60.5 1.3 copy-done.3
  62.0 1.7 scatter-add.21
  63.7 1.1 slice_add_fusion.2
  64.8 0.8 scatter-add.30
  65.7 2.6 fusion.21
  69.1 0.6 mul.156
  69.8 2.4 mul.154
  72.1 28.8 %scatter_custom_fusion.2 = f32[3,16384]{0,1:T(8,128)} fusion(s32[8192]{0:T(1024)S(1)} %broadcast_select_fusion, f32[]{:T(128)} %constant.153.clone.1, f32[3,8192]{0,1:T(8,128)} %bitcast.125, f32[8192]{0:T(1024)S(1)} %mul.156), kind=kCustom, calls=%fused_computation.32 | custom fusion | flops 24576 | bytes 327684
  101.0 6.1 %copy.42 = f32[3,32,512]{2,0,1:T(4,128)} copy(f32[3,32,512]{0,2,1:T(8,128)} %bitcast.124) | data formatting | bytes 393216
  107.2 1.7 scatter-add.24
  109.5 9.2 %all-to-all-start.1 = ((f32[32,3,512]{2,1,0:T(4,128)}), f32[32,3,512]{2,1,0:T(4,128)S(1)}, u32[]{:S(2)}, u32[]{:S(2)}) async-start(f32[32,3,512]{2,1,0:T(4,128)} %bitcast.8), calls=%async_computation.1 | async-start | bytes 524288 | tf_op jit(solution)/shard_map/all_to_all | solution.py:113
  118.8 9.6 %all-to-all-done.1 = f32[32,3,512]{2,1,0:T(4,128)S(1)} async-done(((f32[32,3,512]{2,1,0:T(4,128)}), f32[32,3,512]{2,1,0:T(4,128)S(1)}, u32[]{:S(2)}, u32[]{:S(2)}) %all-to-all-start.1) | async-done | bytes 196640 | tf_op jit(solution)/shard_map/all_to_all | solution.py:113
  128.4 5.1 copy.43
  133.5 94.6 %scatter_custom_fusion = f32[3,20480]{0,1:T(8,128)} fusion(s32[16384]{0:T(1024)S(1)} %bitcast.133, f32[16384,3]{1,0:T(8,128)} %copy.43, f32[]{:T(128)} %constant.153.clone.1), kind=kCustom, calls=%fused_computation.18 | custom fusion | flops 49152 | bytes 246272 | tf_op jit(solution)/shard_map/scatter-add | solution.py:116
  228.0 6.4 %copy.44 = f32[3,8,8,320]{3,2,1,0:T(8,128)S(1)} copy(f32[3,8,8,320]{0,3,2,1:T(8,128)} %bitcast.122) | data formatting | bytes 491520 | tf_op jit(solution)/shard_map/dot_general | solution.py:75
  234.5 5.4 reduce_sum.40
  239.9 322.6 %while.15 = (s32[]{:T(128)}, f32[3,64]{0,1:T(8,128)S(1)}, f32[6,64]{1,0:T(8,128)S(1)}, s32[6,64]{1,0:T(8,128)S(1)}, f32[3,64]{0,1:T(8,128)S(1)}, /*index=5*/f32[64]{0:T(128)S(1)}, s32[]{:T(128)}, s32[]{:T(128)}) while((s32[]{:T(128)}, f32[3,64]{0,1:T(8,128)S(1)}, f32[6,64]{1,0:T(8,128)S(1)}, s32[6,64]{1,0:T(8,128)S(1)}, ...), condition=%wide.region_10.11_spmd.clone, body=%wide.region_8.0_spmd.clone.sunk | while | flops 4867 | bytes 625759 | solution.py:128
  240.0 87.1 %all-gather.3 = f32[256,64,3]{1,2,0:T(4,128)S(1)} all-gather(f32[1,64,3]{1,2,0:T(4,128)S(1)} %select_bitcast_fusion.2), channel_id=1, replica_groups=mesh['group'=32,'span'=8] {'group','span'}, dimensions={0}, use_global_device_ids=true | all-gather | bytes 197376 | tf_op jit(solution)/shard_map/while/body/eval_jaxpr/all_gather | solution.py:124
  327.1 4.8 copy.53
  332.0 4.5 gather_fusion
  336.8 65.6 %all-gather.3 = f32[256,64,3]{1,2,0:T(4,128)S(1)} all-gather(f32[1,64,3]{1,2,0:T(4,128)S(1)} %select_bitcast_fusion.2), channel_id=1, replica_groups=mesh['group'=32,'span'=8] {'group','span'}, dimensions={0}, use_global_device_ids=true | all-gather | bytes 197376 | tf_op jit(solution)/shard_map/while/body/eval_jaxpr/all_gather | solution.py:124
  402.4 4.8 copy.53
  407.2 4.5 gather_fusion
  412.1 65.6 %all-gather.3 = f32[256,64,3]{1,2,0:T(4,128)S(1)} all-gather(f32[1,64,3]{1,2,0:T(4,128)S(1)} %select_bitcast_fusion.2), channel_id=1, replica_groups=mesh['group'=32,'span'=8] {'group','span'}, dimensions={0}, use_global_device_ids=true | all-gather | bytes 197376 | tf_op jit(solution)/shard_map/while/body/eval_jaxpr/all_gather | solution.py:124
  477.6 4.8 copy.53
  482.5 4.5 gather_fusion
  487.3 65.6 %all-gather.3 = f32[256,64,3]{1,2,0:T(4,128)S(1)} all-gather(f32[1,64,3]{1,2,0:T(4,128)S(1)} %select_bitcast_fusion.2), channel_id=1, replica_groups=mesh['group'=32,'span'=8] {'group','span'}, dimensions={0}, use_global_device_ids=true | all-gather | bytes 197376 | tf_op jit(solution)/shard_map/while/body/eval_jaxpr/all_gather | solution.py:124
  552.9 4.8 copy.53
  557.8 4.5 gather_fusion
  562.6 10.6 %convolution_add_fusion = f32[3,8,8,6400]{3,2,1,0:T(8,128)S(1)} fusion(f32[3,8,8,320]{3,2,1,0:T(8,128)S(1)} %copy.44, f32[80,6400]{1,0:T(8,128)} %get-tuple-element.132, f32[80,6400]{1,0:T(8,128)} %get-tuple-element.131, f32[80,6400]{1,0:T(8,128)S(1)} %scatter-add.31, f32[80,6400]{1,0:T(8,128)} %scatter-add.24, f32[6400]{0:T(1024)S(1)} %multiply_multiply_fusion, ...), kind=kOutput, calls=%fused_computation.10 | convolution fusion | flops 4727193600 | bytes 13379328 | tf_op jit(solution)/shard_map/dot_general | solution.py:75
  573.3 5.3 fusion.48
  578.6 0.7 fusion.51
  579.4 2.1 collective-permute-start
  581.4 3.8 collective-permute-start.1
  585.2 5.5 fusion.50
  590.9 1.1 collective-permute-done.1
  592.0 10.9 %fusion.12 = (f32[3,8,8,6400]{3,2,1,0:T(8,128)S(1)}, f32[3,8,8,6400]{3,2,1,0:T(8,128)S(1)}, f32[3,8,8,6400]{3,2,1,0:T(8,128)}) fusion(f32[3,8,8,6400]{3,2,1,0:T(8,128)S(1)} %convolution_add_fusion, f32[3,8,8,1]{3,2,1,0:T(8,128)S(1)} %get-tuple-element.120, f32[3,8,8,6399]{3,2,1,0:T(8,128)} %get-tuple-element.122, f32[3,8,8,6399]{3,2,1,0:T(8,128)} %get-tuple-element.121, ...), kind=kLoop, calls=%fused_computation.26 | loop fusion | flops 19660800 | bytes 40576000 | tf_op jit(solution)/shard_map/mul | solution.py:52
  603.0 3.8 fusion.25
  (89 shorter events, 5.5 us)
Async XLA Ops:
  2.4 13.4 %copy-start.12 = (s32[2]{0:T(128)S(1)}, s32[2]{0:T(128)}, u32[]{:S(2)}) copy-start(s32[2]{0:T(128)} %constant.172) | copy-start | bytes 28
  2.4 13.6 %copy-start.11 = (s32[2]{0:T(128)S(1)}, s32[2]{0:T(128)}, u32[]{:S(2)}) copy-start(s32[2]{0:T(128)} %constant.175) | copy-start | bytes 28
  2.4 13.7 %copy-start.6 = (s32[2048,4]{0,1:T(4,128)S(1)}, s32[2048,4]{0,1:T(4,128)}, u32[]{:S(2)}) copy-start(s32[2048,4]{0,1:T(4,128)} %param.22) | copy-start | bytes 98308
  14.6 51.1 %copy-start.10 = (f32[3,8]{1,0:T(4,128)S(1)}, f32[3,8]{1,0:T(4,128)}, u32[]{:S(2)}) copy-start(f32[3,8]{1,0:T(4,128)} %param.27) | copy-start | bytes 292
  16.5 51.8 %copy-start.7 = (f32[3,2048]{1,0:T(4,128)S(1)}, f32[3,2048]{1,0:T(4,128)}, u32[]{:S(2)}) copy-start(f32[3,2048]{1,0:T(4,128)} %param.19) | copy-start | bytes 73732
  48.2 61.3 %all-to-all-start = ((s32[32,1,512]{2,1,0:T(1,128)}), s32[32,1,512]{2,1,0:T(1,128)S(1)}, u32[]{:S(2)}, u32[]{:S(2)}) async-start(s32[32,1,512]{2,1,0:T(1,128)} %bitcast.2), calls=%async_computation | async-start | bytes 131072 | tf_op jit(solution)/shard_map/all_to_all | solution.py:114
  60.2 8.5 %copy-start.8 = (f32[2048,4]{0,1:T(4,128)S(1)}, f32[2048,4]{0,1:T(4,128)}, u32[]{:S(2)}) copy-start(f32[2048,4]{0,1:T(4,128)} %param.20) | copy-start | bytes 98308
  60.5 1.3 copy-start.3
  65.6 2.8 copy-start.1
  101.0 6.1 %copy-start.9 = (f32[3,64]{1,0:T(4,128)S(1)}, f32[3,64]{1,0:T(4,128)}, u32[]{:S(2)}) copy-start(f32[3,64]{1,0:T(4,128)} %param.23) | copy-start | bytes 2308
  101.0 6.2 %copy-start.4 = (f32[6,64]{1,0:T(8,128)S(1)}, f32[6,64]{1,0:T(8,128)}, u32[]{:S(2)}) copy-start(f32[6,64]{1,0:T(8,128)} %param.24) | copy-start | bytes 4612
  101.0 7.9 %copy-start.2 = (f32[80,6400]{1,0:T(8,128)S(1)}, f32[80,6400]{1,0:T(8,128)}, u32[]{:S(2)}) copy-start(f32[80,6400]{1,0:T(8,128)} %copy-done.1) | copy-start | bytes 6144004
  101.0 8.5 %copy-start.13 = (f32[64]{0:T(128)S(1)}, f32[64]{0:T(128)}, u32[]{:S(2)}) copy-start(f32[64]{0:T(128)} %param.25) | copy-start | bytes 772
  109.5 18.9 %all-to-all-start.1 = ((f32[32,3,512]{2,1,0:T(4,128)}), f32[32,3,512]{2,1,0:T(4,128)S(1)}, u32[]{:S(2)}, u32[]{:S(2)}) async-start(f32[32,3,512]{2,1,0:T(4,128)} %bitcast.8), calls=%async_computation.1 | async-start | bytes 524288 | tf_op jit(solution)/shard_map/all_to_all | solution.py:113
  234.5 5.4 copy-start.5
  573.3 18.7 %copy-start = (f32[3,8,8,6400]{3,2,1,0:T(8,128)}, f32[3,8,8,6400]{3,2,1,0:T(8,128)S(1)}, u32[]{:S(2)}) copy-start(f32[3,8,8,6400]{3,2,1,0:T(8,128)S(1)} %convolution_add_fusion) | copy-start | bytes 14745604
  579.4 11.5 %collective-permute-start = (f32[3,8,1,6400]{3,2,1,0:T(1,128)S(1)}, f32[3,8,1,6400]{3,2,1,0:T(1,128)S(1)}, u32[]{:S(2)}, u32[]{:S(2)}) collective-permute-start(f32[3,8,1,6400]{3,2,1,0:T(1,128)S(1)} %get-tuple-element.127), channel_id=1, source_target_pairs={{1,0},{2,1},{3,2},{4,3},{5,4},{6,5},{7,6},{9,8},{10,9},{11,10},{12... | collective-permute-start | bytes 1843208 | tf_op jit(solution)/shard_map/ppermute | solution.py:20
  581.4 10.6 %collective-permute-start.1 = (f32[3,8,1,6400]{3,2,1,0:T(1,128)S(1)}, f32[3,8,1,6400]{3,2,1,0:T(1,128)S(1)}, u32[]{:S(2)}, u32[]{:S(2)}) collective-permute-start(f32[3,8,1,6400]{3,2,1,0:T(1,128)S(1)} %get-tuple-element.128), channel_id=1, source_target_pairs={{0,1},{1,2},{2,3},{3,4},{4,5},{5,6},{6,7},{8,9},{9,10},{10,11},{11... | collective-permute-start | bytes 1843208 | tf_op jit(solution)/shard_map/ppermute | solution.py:17
where the time goes:
time: 608 us; the launch traced here: 607 us
  blocking collectives  284 us (47%)
  other arithmetic  160 us (26%)
  local copies, waits for them, and re-layouts  113 us (19%)
  starting transfers between devices  26.9 us (4%)
  waiting for transfers between devices  10.7 us (2%)
  matrix products  10.6 us (2%)
    all_gather x4, blocking collectives, sweep(): whole_state = lax.all_gather(state, ('group', 'span'), axis=1, tiled=True)  284 us
    scatter-add x1, other arithmetic, on_device(): empty_faces.at[:, recv_rows.reshape(-1)]  94.6 us
    unnamed x35, local copies, waits for them, and re-layouts  40.8 us
    unnamed x5, other arithmetic  29.2 us
    all_gather x4, local copies, waits for them, and re-layouts, sweep(): whole_state = lax.all_gather(state, ('group', 'span'), axis=1, tiled=True)  19.2 us
    gather x4, local copies, waits for them, and re-layouts, sweep(): neighbours = whole_state[:, skel_edges]  18 us
  transfers between devices with their start and end apart: 4, of which 2 were waited for; matrix products, arithmetic and copies ran while one was open for 9% of the time, Pallas kernels for 0%

commit v1 on v0

v1 whole, which is shorter than its diff:
```python
import functools

import jax
import jax.numpy as jnp
import numpy as np
from jax import lax
from jax.experimental import pallas as pl
from jax.experimental.pallas import tpu as pltpu
from jax.sharding import PartitionSpec as P

F32, BF16, I32 = jnp.float32, jnp.bfloat16, jnp.int32
NP = 80
LAYERS = 64
GROUPS, SPANS = 32, 8
NODES = 2048
MESH = pl.DeviceIdType.MESH
NT = (((1,), (1,)), ((), ()))
VMEM_SPEC = pl.BlockSpec(memory_space=pltpu.VMEM)


def iota(shape, dim):
    return lax.broadcasted_iota(I32, shape, dim)


def split(value):
    high = value.astype(BF16)
    return high, (value - high.astype(F32)).astype(BF16)


def pack_body(disp_ref, weight_ref, owner_ref, row_ref, out_ref, lhs, rhs):
    group_rows = iota((GROUPS, NODES), 0)
    present = jnp.zeros((GROUPS, NODES), F32)
    for t in range(4):
        present += jnp.where(owner_ref[t : t + 1, :] == group_rows, 1.0, 0.0)
    present = present.astype(BF16)
    before = jnp.where(iota((256, 256), 0) < iota((256, 256), 1), 1.0, 0.0).astype(BF16)
    every = jnp.ones((256, 256), BF16)
    base = jnp.zeros((GROUPS, 256), F32)
    ranks = []
    for k in range(NODES // 256):
        piece = present[:, k * 256 : (k + 1) * 256]
        ranks.append(jnp.dot(piece, before, preferred_element_type=F32) + base)
        base += jnp.dot(piece, every, preferred_element_type=F32)
    rank = jnp.concatenate(ranks, axis=1)
    word = iota((8, NODES), 0) & 3
    total = jnp.zeros((512, 256), F32)
    for t in range(4):
        owner = owner_ref[t : t + 1, :]
        slot = jnp.sum(jnp.where(owner == group_rows, rank, 0.0), axis=0, keepdims=True).astype(I32)
        half = slot >> 8
        column = slot & 255
        bucket = owner * 2 + half
        row = row_ref[t : t + 1, :]
        layer = ((row >> 6) * 205) >> 10
        edge = row - layer * (4 * NP)
        seg = ((edge >> 4) * 205) >> 10
        along = (edge - seg * NP) << 8
        line = seg * LAYERS + layer
        weight = weight_ref[t : t + 1, :]
        value = jnp.where(
            word == 0, disp_ref[0:1, :], jnp.where(word == 1, disp_ref[1:2, :], disp_ref[2:3, :])
        ) * weight
        high = jnp.where(word == 3, along.astype(F32), value).astype(BF16)
        low = jnp.where(word == 3, line.astype(F32), value - high.astype(F32)).astype(BF16)
        high = jnp.concatenate([high] * 32, axis=0)
        low = jnp.concatenate([low] * 32, axis=0)
        hit = (iota((256, NODES), 0) >> 2) == bucket
        zero = jnp.zeros((), BF16)
        lhs[0:256, :] = jnp.where(hit, high, zero)
        lhs[256:512, :] = jnp.where(hit, low, zero)
        rhs[...] = jnp.where(iota((256, NODES), 0) == column, 1.0, 0.0).astype(BF16)
        total += lax.dot_general(lhs[...], rhs[...], NT, preferred_element_type=F32)
    out_ref[...] = (total[0:256] + total[256:512]).reshape(GROUPS, 8, 256)


def pack(disp, weight, owner, row):
    return pl.pallas_call(
        pack_body,
        name="pack",
        out_shape=jax.ShapeDtypeStruct((GROUPS, 8, 256), F32),
        in_specs=[VMEM_SPEC] * 4,
        out_specs=VMEM_SPEC,
        scratch_shapes=[pltpu.VMEM((512, NODES), BF16), pltpu.VMEM((256, NODES), BF16)],
        compiler_params=pltpu.CompilerParams(vmem_limit_bytes=48 << 20),
    )(disp, weight, owner, row)


def wait_for(ref, sem):
    pltpu.make_async_copy(ref, ref, sem).wait()


def exchange_body(send_ref, recv_ref, send_sem, recv_sem, own_sem):
    g, s = lax.axis_index("group"), lax.axis_index("span")
    barrier = pltpu.get_barrier_semaphore()

    def greet(k, carry):
        pl.semaphore_signal(barrier, inc=1, device_id=((g + k) % GROUPS, s), device_id_type=MESH)
        return carry

    lax.fori_loop(1, GROUPS, greet, 0)
    pl.semaphore_wait(barrier, GROUPS - 1)
    own = pltpu.make_async_copy(send_ref.at[g], recv_ref.at[g], own_sem)
    own.start()

    def push(k, carry):
        peer = (g + k) % GROUPS
        pltpu.make_async_remote_copy(
            send_ref.at[peer],
            recv_ref.at[g],
            send_sem,
            recv_sem,
            device_id=(peer, s),
            device_id_type=MESH,
        ).start()
        return carry

    lax.fori_loop(1, GROUPS, push, 0)
    own.wait()
    wait_for(recv_ref.at[pl.ds(0, GROUPS - 1)], recv_sem)
    wait_for(send_ref.at[pl.ds(0, GROUPS - 1)], send_sem)


def exchange(send):
    return pl.pallas_call(
        exchange_body,
        name="exchange",
        out_shape=jax.ShapeDtypeStruct((GROUPS, 8, 256), F32),
        in_specs=[VMEM_SPEC],
        out_specs=VMEM_SPEC,
        scratch_shapes=[pltpu.SemaphoreType.DMA] * 3,
        compiler_params=pltpu.CompilerParams(collective_id=0, has_side_effects=True),
    )(send)


def gather_body(recv_ref, force_ref, coupling_ref, stiff_ref, faces_ref, first_ref, total):
    total[...] = jnp.zeros_like(total)
    lines = iota((256, 256), 0)
    places = iota((NP, 256), 0)
    zero = jnp.zeros((), BF16)

    def add(g, carry):
        lhs, rhs = [], []
        for h in range(2):
            code = recv_ref[g, 4 * h + 3 : 4 * h + 4, :].astype(I32)
            hit = places == (code >> 8)
            parts = []
            for c in range(3):
                for part in split(recv_ref[g, 4 * h + c : 4 * h + c + 1, :]):
                    parts.append(jnp.where(hit, jnp.broadcast_to(part, (NP, 256)), zero))
            lhs.append(jnp.concatenate(parts, axis=0))
            rhs.append(jnp.where(lines == (code & 255), 1.0, 0.0).astype(BF16))
        total[...] += lax.dot_general(
            jnp.concatenate(lhs, axis=1), jnp.concatenate(rhs, axis=1), NT, preferred_element_type=F32
        )
        return carry

    lax.fori_loop(0, GROUPS, add, 0)
    diagonal = stiff_ref[...] + jnp.sum(coupling_ref[...], axis=0, keepdims=True)
    row = iota((8, 128), 0)
    first = jnp.zeros((8, 128), F32)
    for c in range(3):
        sums = total[2 * c * NP : (2 * c + 1) * NP, :] + total[(2 * c + 1) * NP : (2 * c + 2) * NP, :]
        load = jnp.sum(sums, axis=0, keepdims=True)
        load = load[:, 0:128] + load[:, 128:256]
        load = load + pltpu.roll(load, 64, axis=1)
        value = (force_ref[c : c + 1, :] + 0.25 * load[:, 0:64]) / diagonal
        first = jnp.where(row == c, jnp.concatenate([value, value], axis=1), first)
        full = jnp.concatenate([sums, jnp.zeros((128 - NP, 256), F32)], axis=0)
        faces_ref[c] = full.T
    first_ref[...] = first


def add_up(recv, force, coupling, stiff):
    return pl.pallas_call(
        gather_body,
        name="add_up",
        out_shape=(
            jax.ShapeDtypeStruct((3, 256, 128), F32),
            jax.ShapeDtypeStruct((8, 128), F32),
        ),
        in_specs=[VMEM_SPEC] * 4,
        out_specs=(VMEM_SPEC, VMEM_SPEC),
        scratch_shapes=[pltpu.VMEM((6 * NP, 256), F32)],
        compiler_params=pltpu.CompilerParams(vmem_limit_bytes=48 << 20),
    )(recv, force, coupling, stiff)


ROUNDS = 3


def sweep_body(
    first_ref, coupling_ref, stiff_ref, edges_ref, faces_ref,
    skel_ref, low_ref, high_ref,
    static, low_in, high_in, face_out, near, far, picks, weights,
    near_send, near_recv, far_send, far_recv, halo_send, halo_recv,
):
    g, s = lax.axis_index("group"), lax.axis_index("span")
    barrier = pltpu.get_barrier_semaphore()

    def greet_group(k, carry):
        pl.semaphore_signal(barrier, inc=1, device_id=((g + k) % GROUPS, s), device_id_type=MESH)
        return carry

    def greet_span(k, carry):
        pl.semaphore_signal(barrier, inc=1, device_id=(g, (s + k) % SPANS), device_id_type=MESH)
        return carry

    lax.fori_loop(1, GROUPS, greet_group, 0)
    lax.fori_loop(1, SPANS, greet_span, 0)

    lane = iota((8, 128), 1)
    own_half = lane < 64
    diagonal = stiff_ref[...] + jnp.sum(coupling_ref[...], axis=0, keepdims=True)
    share = coupling_ref[...] / diagonal
    blank = jnp.zeros((6, 64), F32)
    static[0:6, :] = jnp.concatenate([share, blank], axis=1)
    static[8:14, :] = jnp.concatenate([edges_ref[...].astype(F32), blank], axis=1)
    static[16:24, :] = first_ref[...]
    for c in range(3):
        face_out[0, c] = faces_ref[c, pl.ds(7, 32, stride=8), :]
        face_out[1, c] = faces_ref[c, pl.ds(0, 32, stride=8), :]

    def place(state):
        state = jnp.where(own_half, state, 0.0)
        return jnp.where(g % 2 == 1, pltpu.roll(state, 64, axis=1), state)[0:4, :]

    near[0, g] = place(first_ref[...])
    pl.semaphore_wait(barrier, GROUPS - 1 + SPANS - 1)

    def push_near(r):
        def push(k, carry):
            peer = (g + k) % GROUPS
            pltpu.make_async_remote_copy(
                near.at[r, g], near.at[r, g], near_send.at[r], near_recv.at[r],
                device_id=(peer, s), device_id_type=MESH,
            ).start()
            return carry

        lax.fori_loop(1, GROUPS, push, 0)

    push_near(0)
    up, down = (s + 1) % SPANS, (s + SPANS - 1) % SPANS
    halos = [
        pltpu.make_async_remote_copy(
            src, dst, halo_send.at[n], halo_recv.at[n], device_id=(g, to), device_id_type=MESH
        )
        for n, (src, dst, to) in enumerate(
            [
                (static, low_in, up),
                (static, high_in, down),
                (face_out.at[0], low_ref, up),
                (face_out.at[1], high_ref, down),
            ]
        )
    ]
    for halo in halos:
        halo.start()
    halos[0].wait_recv()
    halos[1].wait_recv()
    turn = lane & 7

    def extended(rows):
        beyond = jnp.where(turn == 7, low_in[rows, :], jnp.where(turn == 0, high_in[rows, :], 0.0))
        return jnp.where(own_half, static[rows, :], pltpu.roll(beyond, 64, axis=1))

    share = extended(slice(0, 8))
    edges = extended(slice(8, 16)).astype(I32)
    first = extended(slice(16, 24))
    for d in range(6):
        node = edges[d : d + 1, :]
        group, span, local = node >> 9, (node >> 6) & 7, node & 63
        column = (group & 1) * 64 + local
        pick = jnp.where(iota((128, 128), 0) == column, 1.0, 0.0).astype(BF16)
        cols = slice(d * 128, (d + 1) * 128)
        picks[0:128, cols] = pick
        picks[128:256, cols] = pick
        line = span * 16 + (group >> 1)
        weights[:, cols] = jnp.where(iota((128, 128), 0) == line, share[d : d + 1, :], 0.0)
    row = iota((8, 128), 0)
    state = first
    for r in range(ROUNDS):
        wait_for(near.at[r, pl.ds(0, GROUPS - 1)], near_recv.at[r])
        for h in range(16):
            pair = near[r, 2 * h] + near[r, 2 * h + 1]
            for c in range(3):
                far[r, s, c * 16 + h : c * 16 + h + 1, :] = pair[c : c + 1, :]

        def push(k, carry):
            peer = (s + k) % SPANS
            pltpu.make_async_remote_copy(
                far.at[r, s], far.at[r, s], far_send.at[r], far_recv.at[r],
                device_id=(g, peer), device_id_type=MESH,
            ).start()
            return carry

        lax.fori_loop(1, SPANS, push, 0)
        wait_for(far.at[r, pl.ds(0, SPANS - 1)], far_recv.at[r])
        table = far[r].reshape(SPANS * 48, 128)
        found = jnp.dot(jnp.concatenate(split(table), axis=1), picks[...], preferred_element_type=F32)
        found = found.reshape(SPANS, 3, 16, 768)
        weighted = weights[...].reshape(SPANS, 16, 768)
        state = first
        for c in range(3):
            total = jnp.sum((found[:, c] * weighted).reshape(SPANS * 16, 768), axis=0, keepdims=True)
            parts = [total[:, d * 128 : (d + 1) * 128] for d in range(6)]
            state = state + jnp.where(row == c, functools.reduce(jnp.add, parts), 0.0)
        if r + 1 < ROUNDS:
            near[r + 1, g] = place(state)
            push_near(r + 1)
    skel_ref[...] = state
    halos[2].wait_recv()
    halos[3].wait_recv()
    for halo in halos:
        halo.wait_send()
    for r in range(ROUNDS):
        wait_for(near.at[r, pl.ds(0, GROUPS - 1)], near_send.at[r])
        wait_for(far.at[r, pl.ds(0, SPANS - 1)], far_send.at[r])


def sweeps(first, coupling, stiff, edges, faces):
    dma = pltpu.SemaphoreType.DMA
    return pl.pallas_call(
        sweep_body,
        name="sweeps",
        out_shape=(
            jax.ShapeDtypeStruct((8, 128), F32),
            jax.ShapeDtypeStruct((3, 32, 128), F32),
            jax.ShapeDtypeStruct((3, 32, 128), F32),
        ),
        in_specs=[VMEM_SPEC] * 5,
        out_specs=(VMEM_SPEC,) * 3,
        scratch_shapes=[
            pltpu.VMEM((24, 128), F32),
            pltpu.VMEM((24, 128), F32),
            pltpu.VMEM((24, 128), F32),
            pltpu.VMEM((2, 3, 32, 128), F32),
            pltpu.VMEM((ROUNDS, GROUPS, 4, 128), F32),
            pltpu.VMEM((ROUNDS, SPANS, 48, 128), F32),
            pltpu.VMEM((256, 768), BF16),
            pltpu.VMEM((128, 768), F32),
            dma((ROUNDS,)), dma((ROUNDS,)), dma((ROUNDS,)), dma((ROUNDS,)), dma((4,)), dma((4,)),
        ],
        compiler_params=pltpu.CompilerParams(
            collective_id=1, has_side_effects=True, vmem_limit_bytes=48 << 20
        ),
    )(first, coupling, stiff, edges, faces)


def blend_tables():
    f = np.arange(NP * NP)
    i, j = f % NP, f // NP
    n = NP - 1
    s, t = i / n, j / n

    def bubble(i, j):
        s, t = i / n, j / n
        return 16.0 * s * (1 - s) * t * (1 - t)

    ip, im = np.minimum(i + 1, n), np.maximum(i - 1, 0)
    jp, jm = np.minimum(j + 1, n), np.maximum(j - 1, 0)
    rows = [
        s, t, (ip - im) / (2.0 * n), (jp - jm) / (2.0 * n),
        bubble(i, j), 0.5 * (bubble(ip, j) - bubble(im, j)), 0.5 * (bubble(i, jp) - bubble(i, jm)),
    ]
    rows.append(np.zeros_like(s))
    return np.stack(rows).astype(np.float32), np.stack([i, j] + [i] * 6).astype(np.int32)


def pick_lanes(x, index):
    return jnp.take_along_axis(x, index, axis=1)


def blend_body(spacing_ref, faces_ref, low_ref, high_ref, skel_ref, table_ref, index_ref, disp_ref, jac_ref):
    q = pl.program_id(0)
    span = lax.axis_index("span")
    has_low = jnp.where(span > 0, 1.0, 0.0).astype(F32)
    has_high = jnp.where(span < SPANS - 1, 1.0, 0.0).astype(F32)
    row, lane = iota((8, 128), 0), iota((8, 128), 1)
    frac = lane.astype(F32) * (1.0 / (NP - 1))

    def along_span(x, before, after):
        nxt = jnp.where(row == 7, after * has_high, pltpu.roll(x, 7, axis=0))
        prv = jnp.where(row == 0, before * has_low, pltpu.roll(x, 1, axis=0))
        return 0.5 * (nxt - prv)

    def along_lane(x):
        nxt = jnp.where(lane == NP - 1, x, pltpu.roll(x, 127, axis=1))
        prv = jnp.where(lane == 0, x, pltpu.roll(x, 1, axis=1))
        return 0.5 * (nxt - prv)

    def inner(x):
        return x - (1.0 - frac) * x[:, 0:1] - frac * x[:, NP - 1 : NP]

    lane_fns, column_fns, bumps = [], [], []
    for c in range(3):
        now, diff = [], []
        for seg in range(4):
            x = faces_ref[c, pl.ds(pl.multiple_of(seg * LAYERS + q * 8, 8), 8), :]
            before = low_ref[c, pl.ds(seg * 8 + q, 1), :]
            after = high_ref[c, pl.ds(seg * 8 + q, 1), :]
            now.append(x)
            diff.append(along_span(x, before, after))
        values = []
        for bottom, top, left, right in (now, diff):
            base = inner(bottom)
            values.append((base, inner(top) - base, left, right - left))
        (b, d, left, m), (b_s, d_s, left_s, m_s) = values
        lane_fns.append((b, d, along_lane(b), along_lane(d), b_s, d_s))
        column_fns.append((left, m, along_lane(left), along_lane(m), left_s, m_s))
        skel = jnp.broadcast_to(skel_ref[c : c + 1, :], (8, 128))

        def column(where):
            return jnp.sum(jnp.where(where, skel, 0.0), axis=1, keepdims=True)

        value = column(lane == q * 8 + row)
        nxt = column(lane == jnp.where(row == 7, 64 + q * 8, q * 8 + row + 1))
        prv = column(lane == jnp.where(row == 0, 64 + q * 8 + 7, q * 8 + row - 1))
        nxt = jnp.where(row == 7, nxt * has_high, nxt)
        prv = jnp.where(row == 0, prv * has_low, prv)
        bumps.append((jnp.broadcast_to(value, (8, 128)), 0.5 * (nxt - prv)))
    spacing = [spacing_ref[c, q] for c in range(3)]

    for phase in range(5):
        where = jnp.broadcast_to(index_ref[0:1, phase * 128 : (phase + 1) * 128], (8, 128))
        lanes = [[pick_lanes(x, where) for x in fns] for fns in lane_fns]
        for turn in range(10):
            cols = slice((turn * 5 + phase) * 128, (turn * 5 + phase + 1) * 128)
            where = jnp.broadcast_to(index_ref[1:2, cols], (8, 128))
            s, t, s_i, t_j, bump, bump_i, bump_j = [table_ref[n : n + 1, cols] for n in range(7)]
            matrix = []
            for c in range(3):
                b, d, b_i, d_i, b_s, d_s = lanes[c]
                left, m, left_j, m_j, left_s, m_s = [pick_lanes(x, where) for x in column_fns[c]]
                k, k_s = bumps[c]
                disp_ref[c, 0, :, cols] = b + t * d + left + s * m + bump * k
                matrix.append(
                    [
                        b_i + t * d_i + s_i * m + bump_i * k,
                        t_j * d + left_j + s * m_j + bump_j * k,
                        b_s + t * d_s + left_s + s * m_s + bump * k_s,
                    ]
                )
                matrix[c][c] = matrix[c][c] + spacing[c]
            one = matrix[1][1] * matrix[2][2] - matrix[1][2] * matrix[2][1]
            two = matrix[1][0] * matrix[2][2] - matrix[1][2] * matrix[2][0]
            three = matrix[1][0] * matrix[2][1] - matrix[1][1] * matrix[2][0]
            jac_ref[0, :, cols] = matrix[0][0] * one - matrix[0][1] * two + matrix[0][2] * three


def blend(spacing, faces, low, high, skel):
    table, index = blend_tables()
    whole = lambda *shape: pl.BlockSpec(shape, lambda q: (0,) * len(shape))
    return pl.pallas_call(
        blend_body,
        name="blend",
        grid=(8,),
        out_shape=(
            jax.ShapeDtypeStruct((3, 8, 8, NP * NP), F32),
            jax.ShapeDtypeStruct((8, 8, NP * NP), F32),
        ),
        in_specs=[
            pl.BlockSpec(memory_space=pltpu.SMEM),
            whole(3, 256, 128),
            whole(3, 32, 128),
            whole(3, 32, 128),
            whole(8, 128),
            whole(8, NP * NP),
            whole(8, NP * NP),
        ],
        out_specs=(
            pl.BlockSpec((3, 1, 8, NP * NP), lambda q: (0, q, 0, 0)),
            pl.BlockSpec((1, 8, NP * NP), lambda q: (q, 0, 0)),
        ),
        compiler_params=pltpu.CompilerParams(
            dimension_semantics=("arbitrary",), vmem_limit_bytes=48 << 20
        ),
    )(spacing, faces, low, high, skel, jnp.asarray(table), jnp.asarray(index))


def on_device(disp, weight, owner, row, force, coupling, stiff, edges, spacing):
    stiff = stiff.reshape(1, -1)
    send = pack(disp, weight.T, owner.T, row.T)
    recv = exchange(send)
    faces, first = add_up(recv, force, coupling, stiff)
    skel, low, high = sweeps(first, coupling, stiff, edges, faces)
    return blend(spacing, faces, low, high, skel)


def solution(mesh):
    return jax.shard_map(
        on_device,
        mesh=mesh,
        in_specs=(
            P(None, ("group", "span")),
            P(("group", "span"), None),
            P(("group", "span"), None),
            P(("group", "span"), None),
            P(None, ("group", "span")),
            P(None, ("group", "span")),
            P(("group", "span")),
            P(None, ("group", "span")),
            P(None, "group"),
        ),
        out_specs=(P(None, "group", "span", None), P("group", "span", None)),
        check_vma=False,
    )
```

time: 608 us -> 98.6 us (0.16)
  blocking collectives: 284 us -> 0 us
  other arithmetic: 160 us -> 0 us
  local copies, waits for them, and re-layouts: 113 us -> 9.9 us
  Pallas kernels: 0 us -> 87.4 us
  starting transfers between devices: 26.9 us -> 0 us
  waiting for transfers between devices: 10.7 us -> 0 us
  matrix products: 10.6 us -> 0 us
    all_gather x4 -> x0, blocking collectives: 284 us -> none  [sweep(): whole_state = lax.all_gather(state, ('group', 'span'), axis=1, tiled=True)]
    scatter-add x1 -> x0, other arithmetic: 94.6 us -> none  [on_device(): empty_faces.at[:, recv_rows.reshape(-1)]]
    pallas_call x0 -> x5, Pallas kernels: none -> 87.4 us  [the longest x1 40.2 us: sweeps(): pl.pallas_call(sweep_body, name='sweeps', out_shape=(jax.ShapeDtypeStruct...]
    unnamed x35 -> x26, local copies, waits for them, and re-layouts: 40.8 us -> 9.9 us
    unnamed x5 -> x0, other arithmetic: 29.2 us -> none
    all_to_all x2 -> x0, starting transfers between devices: 21.1 us -> none  [the longest x1 11.9 us: on_device(): lax.all_to_all(send_rows, 'group', split_axis=0, concat_axis=0, tiled=True)]
    all_gather x4 -> x0, local copies, waits for them, and re-layouts: 19.2 us -> none  [sweep(): whole_state = lax.all_gather(state, ('group', 'span'), axis=1, tiled=True)]
    gather x4 -> x0, local copies, waits for them, and re-layouts: 18 us -> none  [sweep(): neighbours = whole_state[:, skel_edges]]
  transfers between devices with their start and end apart: 4 -> 0, of which waited for: 2 -> 0; matrix products, arithmetic and copies ran while one was open for 9% -> 0% of each run, Pallas kernels for 0% -> 0%
where the time goes in v1:
time: 98.6 us; the launch traced here: 98 us
  Pallas kernels  87.4 us (89%)
  local copies, waits for them, and re-layouts  9.9 us (10%)
    pallas_call x1, Pallas kernels, sweeps(): pl.pallas_call(sweep_body, name='sweeps', out_shape=(jax.ShapeDtypeStruct...  40.2 us
    pallas_call x1, Pallas kernels, exchange(): pl.pallas_call(exchange_body, name='exchange', out_shape=jax.ShapeDtypeSt...  18.4 us
    pallas_call x1, Pallas kernels, blend(): pl.pallas_call(blend_body, name='blend', grid=(8,), out_shape=(jax.ShapeD...  14.3 us
    pallas_call x1, Pallas kernels, add_up(): pl.pallas_call(gather_body, name='add_up', out_shape=(jax.ShapeDtypeStruc...  11.1 us
    unnamed x26, local copies, waits for them, and re-layouts  9.9 us
    pallas_call x1, Pallas kernels, pack(): pl.pallas_call(pack_body, name='pack', out_shape=jax.ShapeDtypeStruct((GR...  3.42 us

profile of v1, /device:TPU:1, one launch (start us, length us, event | category | flops | bytes accessed | tf_op | source)
XLA Modules:
  0.0 98.0 jit_solution(17130690446268932964)
XLA Ops:
  0.6 0.0 copy-start.4
  0.6 0.7 copy-done.4
  1.4 0.0 copy-start.5
  1.4 0.8 copy-done.5
  2.1 0.0 copy-start.6
  2.1 0.8 copy-done.6
  2.9 0.0 copy-start.7
  2.9 0.8 copy-done.7
  3.7 3.4 %pack.1.send_ref = f32[32,8,256]{2,1,0:T(8,128)S(1)} custom-call(f32[3,2048]{1,0:T(4,128)S(1)} %copy-done.4, f32[4,2048]{1,0:T(4,128)S(1)} %bitcast.4, s32[4,2048]{1,0:T(4,128)S(1)} %bitcast.5, s32[4,2048]{1,0:T(4,128)S(1)} %bitcast.6), custom_call_target="tpu_custom_call" | custom-call | tf_op jit(solution)/shard_map/pack/pallas_call | solution.py:77
  7.1 0.0 copy-start.1
  7.1 0.7 copy-done.1
  7.8 18.4 %exchange.1.recv_ref = f32[32,8,256]{2,1,0:T(8,128)} custom-call(f32[32,8,256]{2,1,0:T(8,128)} %copy-done.1), custom_call_target="tpu_custom_call" | custom-call | tf_op jit(solution)/shard_map/exchange/pallas_call | solution.py:124
  26.2 0.0 copy-start
  26.2 0.9 copy-done
  27.1 0.0 copy-start.8
  27.1 0.7 copy-done.8
  27.8 0.0 copy-start.10
  27.8 0.7 copy-done.10
  28.5 0.0 copy-start.12
  28.5 0.7 copy-done.12
  29.2 11.1 %add_up.1 = (f32[3,256,128]{2,1,0:T(8,128)S(1)}, f32[8,128]{1,0:T(8,128)S(1)}) custom-call(f32[32,8,256]{2,1,0:T(8,128)S(1)} %copy-done, f32[3,64]{1,0:T(4,128)S(1)} %copy-done.10, f32[6,64]{1,0:T(8,128)S(1)} %copy-done.8, f32[1,64]{1,0:T(1,128)S(1)} %bitcast.7), custom_call_target="tpu_custom_call" | custom-call | tf_op jit(solution)/shard_map/add_up/pallas_call | solution.py:174
  40.3 0.0 copy-start.9
  40.3 0.7 copy-done.9
  40.9 40.2 %sweeps.1 = (f32[8,128]{1,0:T(8,128)S(1)}, f32[3,32,128]{2,1,0:T(8,128)S(1)}, f32[3,32,128]{2,1,0:T(8,128)S(1)}) custom-call(f32[8,128]{1,0:T(8,128)S(1)} %get-tuple-element.8.first_ref, f32[6,64]{1,0:T(8,128)S(1)} %copy-done.8, f32[1,64]{1,0:T(1,128)S(1)} %bitcast.8, s32[6,64]{1,0:T(8,128)S(1)} %copy-done.9, f32[3,256,128]{2,1,0:T(8,128)S(1)} %get-tuple-element.7.faces_ref), custom_call_target="tpu_custom_call" | custom-call | tf_op jit(solution)/shard_map/sweeps/pallas_call | solution.py:322
  81.2 0.0 copy-start.2
  81.2 0.9 copy-done.2
  82.1 0.0 copy-start.3
  82.1 0.9 copy-done.3
  83.0 0.0 copy-start.11
  83.0 0.7 copy-done.11
  83.7 14.3 %blend.1 = (f32[3,8,8,6400]{3,2,1,0:T(8,128)}, f32[8,8,6400]{2,1,0:T(8,128)}) custom-call(f32[3,8]{1,0:T(4,128)S(1)} %copy-done.11, f32[3,256,128]{2,1,0:T(8,128)S(1)} %get-tuple-element.7.faces_ref, f32[3,32,128]{2,1,0:T(8,128)S(1)} %get-tuple-element.9.low_ref, f32[3,32,128]{2,1,0:T(8,128)S(1)} %get-tuple-element.10.high_ref, ...), custom_call_target="tpu_custom_call" | custom-call | tf_op jit(solution)/shard_map/blend/pallas_call | solution.py:453
Async XLA Ops:
  0.6 0.8 copy-start.4
  1.4 0.8 copy-start.5
  2.1 0.8 copy-start.6
  2.9 0.8 copy-start.7
  7.1 0.7 copy-start.1
  26.2 1.0 copy-start
  27.1 0.7 copy-start.8
  27.8 0.7 copy-start.10
  28.5 0.7 copy-start.12
  40.3 0.7 copy-start.9
  81.2 0.9 copy-start.2
  82.1 0.9 copy-start.3
  83.0 0.7 copy-start.11

commit v2 on v1

--- a/solution.py
+++ b/solution.py
@@ -27,7 +27,18 @@
     return high, (value - high.astype(F32)).astype(BF16)
 
 
-def pack_body(disp_ref, weight_ref, owner_ref, row_ref, out_ref, lhs, rhs):
+def wait_for(ref, sem):
+    pltpu.make_async_copy(ref, ref, sem).wait()
+
+
+def offset_peer(g, k):
+    n, m = k // 4, k % 4
+    dz = 4 + ((n + 1) // 2) * (1 - 2 * (n % 2))
+    dx = 2 + ((m + 1) // 2) * (1 - 2 * (m % 2))
+    return ((g // 8 + dx) % 4) * 8 + (g % 8 + dz) % 8
+
+
+def pack(disp_ref, weight_ref, owner_ref, row_ref, out_ref, lhs, rhs):
     group_rows = iota((GROUPS, NODES), 0)
     present = jnp.zeros((GROUPS, NODES), F32)
     for t in range(4):
@@ -73,199 +84,109 @@
     out_ref[...] = (total[0:256] + total[256:512]).reshape(GROUPS, 8, 256)
 
 
-def pack(disp, weight, owner, row):
-    return pl.pallas_call(
-        pack_body,
-        name="pack",
-        out_shape=jax.ShapeDtypeStruct((GROUPS, 8, 256), F32),
-        in_specs=[VMEM_SPEC] * 4,
-        out_specs=VMEM_SPEC,
-        scratch_shapes=[pltpu.VMEM((512, NODES), BF16), pltpu.VMEM((256, NODES), BF16)],
-        compiler_params=pltpu.CompilerParams(vmem_limit_bytes=48 << 20),
-    )(disp, weight, owner, row)
-
-
-def wait_for(ref, sem):
-    pltpu.make_async_copy(ref, ref, sem).wait()
-
-
-def exchange_body(send_ref, recv_ref, send_sem, recv_sem, own_sem):
-    g, s = lax.axis_index("group"), lax.axis_index("span")
-    barrier = pltpu.get_barrier_semaphore()
-
-    def greet(k, carry):
-        pl.semaphore_signal(barrier, inc=1, device_id=((g + k) % GROUPS, s), device_id_type=MESH)
-        return carry
-
-    lax.fori_loop(1, GROUPS, greet, 0)
-    pl.semaphore_wait(barrier, GROUPS - 1)
-    own = pltpu.make_async_copy(send_ref.at[g], recv_ref.at[g], own_sem)
-    own.start()
-
-    def push(k, carry):
-        peer = (g + k) % GROUPS
-        pltpu.make_async_remote_copy(
-            send_ref.at[peer],
-            recv_ref.at[g],
-            send_sem,
-            recv_sem,
-            device_id=(peer, s),
-            device_id_type=MESH,
-        ).start()
-        return carry
-
-    lax.fori_loop(1, GROUPS, push, 0)
-    own.wait()
-    wait_for(recv_ref.at[pl.ds(0, GROUPS - 1)], recv_sem)
-    wait_for(send_ref.at[pl.ds(0, GROUPS - 1)], send_sem)
-
-
-def exchange(send):
-    return pl.pallas_call(
-        exchange_body,
-        name="exchange",
-        out_shape=jax.ShapeDtypeStruct((GROUPS, 8, 256), F32),
-        in_specs=[VMEM_SPEC],
-        out_specs=VMEM_SPEC,
-        scratch_shapes=[pltpu.SemaphoreType.DMA] * 3,
-        compiler_params=pltpu.CompilerParams(collective_id=0, has_side_effects=True),
-    )(send)
-
-
-def gather_body(recv_ref, force_ref, coupling_ref, stiff_ref, faces_ref, first_ref, total):
-    total[...] = jnp.zeros_like(total)
+def add_up(recv_ref, sources):
     lines = iota((256, 256), 0)
     places = iota((NP, 256), 0)
     zero = jnp.zeros((), BF16)
-
-    def add(g, carry):
-        lhs, rhs = [], []
+    lhs, rhs = [], []
+    for source in sources:
         for h in range(2):
-            code = recv_ref[g, 4 * h + 3 : 4 * h + 4, :].astype(I32)
+            code = recv_ref[source, 4 * h + 3 : 4 * h + 4, :].astype(I32)
             hit = places == (code >> 8)
             parts = []
             for c in range(3):
-                for part in split(recv_ref[g, 4 * h + c : 4 * h + c + 1, :]):
+                for part in split(recv_ref[source, 4 * h + c : 4 * h + c + 1, :]):
                     parts.append(jnp.where(hit, jnp.broadcast_to(part, (NP, 256)), zero))
             lhs.append(jnp.concatenate(parts, axis=0))
             rhs.append(jnp.where(lines == (code & 255), 1.0, 0.0).astype(BF16))
-        total[...] += lax.dot_general(
-            jnp.concatenate(lhs, axis=1), jnp.concatenate(rhs, axis=1), NT, preferred_element_type=F32
-        )
-        return carry
-
-    lax.fori_loop(0, GROUPS, add, 0)
-    diagonal = stiff_ref[...] + jnp.sum(coupling_ref[...], axis=0, keepdims=True)
-    row = iota((8, 128), 0)
-    first = jnp.zeros((8, 128), F32)
-    for c in range(3):
-        sums = total[2 * c * NP : (2 * c + 1) * NP, :] + total[(2 * c + 1) * NP : (2 * c + 2) * NP, :]
-        load = jnp.sum(sums, axis=0, keepdims=True)
-        load = load[:, 0:128] + load[:, 128:256]
-        load = load + pltpu.roll(load, 64, axis=1)
-        value = (force_ref[c : c + 1, :] + 0.25 * load[:, 0:64]) / diagonal
-        first = jnp.where(row == c, jnp.concatenate([value, value], axis=1), first)
-        full = jnp.concatenate([sums, jnp.zeros((128 - NP, 256), F32)], axis=0)
-        faces_ref[c] = full.T
-    first_ref[...] = first
-
-
-def add_up(recv, force, coupling, stiff):
-    return pl.pallas_call(
-        gather_body,
-        name="add_up",
-        out_shape=(
-            jax.ShapeDtypeStruct((3, 256, 128), F32),
-            jax.ShapeDtypeStruct((8, 128), F32),
-        ),
-        in_specs=[VMEM_SPEC] * 4,
-        out_specs=(VMEM_SPEC, VMEM_SPEC),
-        scratch_shapes=[pltpu.VMEM((6 * NP, 256), F32)],
-        compiler_params=pltpu.CompilerParams(vmem_limit_bytes=48 << 20),
-    )(recv, force, coupling, stiff)
+    return lax.dot_general(
+        jnp.concatenate(lhs, axis=1), jnp.concatenate(rhs, axis=1), NT, preferred_element_type=F32
+    )
 
 
 ROUNDS = 3
-
-
-def sweep_body(
-    first_ref, coupling_ref, stiff_ref, edges_ref, faces_ref,
-    skel_ref, low_ref, high_ref,
+TOGETHER = 4
+
+
+def front_body(
+    disp_hbm, weight_hbm, owner_hbm, row_hbm, force_hbm, coupling_hbm, stiff_hbm, edges_hbm,
+    faces_ref, skel_ref, low_ref, high_ref,
+    disp_ref, weight_ref, owner_ref, row_ref, force_ref, coupling_ref, stiff_ref, edges_ref,
+    lhs, rhs, send, recv, total, first_ref, first_low, first_high,
     static, low_in, high_in, face_out, near, far, picks, weights,
-    near_send, near_recv, far_send, far_recv, halo_send, halo_recv,
+    load_sem, send_sem, recv_sem, near_send, near_recv, far_send, far_recv, halo_send, halo_recv,
 ):
     g, s = lax.axis_index("group"), lax.axis_index("span")
+    up, down = (s + 1) % SPANS, (s + SPANS - 1) % SPANS
+    loads = [
+        pltpu.make_async_copy(src, dst, load_sem.at[n])
+        for n, (src, dst) in enumerate(
+            [
+                (owner_hbm, owner_ref), (row_hbm, row_ref), (disp_hbm, disp_ref), (weight_hbm, weight_ref),
+                (coupling_hbm, coupling_ref), (stiff_hbm, stiff_ref), (edges_hbm, edges_ref), (force_hbm, force_ref),
+            ]
+        )
+    ]
+    for load in loads:
+        load.start()
     barrier = pltpu.get_barrier_semaphore()
 
     def greet_group(k, carry):
-        pl.semaphore_signal(barrier, inc=1, device_id=((g + k) % GROUPS, s), device_id_type=MESH)
+        pl.semaphore_signal(barrier, inc=1, device_id=(offset_peer(g, k), s), device_id_type=MESH)
         return carry
 
     def greet_span(k, carry):
         pl.semaphore_signal(barrier, inc=1, device_id=(g, (s + k) % SPANS), device_id_type=MESH)
         return carry
 
-    lax.fori_loop(1, GROUPS, greet_group, 0)
+    lax.fori_loop(0, GROUPS - 1, greet_group, 0)
     lax.fori_loop(1, SPANS, greet_span, 0)
-
-    lane = iota((8, 128), 1)
-    own_half = lane < 64
+    for load in loads:
+        load.wait()
+    pack(disp_ref, weight_ref, owner_ref, row_ref, send, lhs, rhs)
+    recv[g] = send[g]
     diagonal = stiff_ref[...] + jnp.sum(coupling_ref[...], axis=0, keepdims=True)
-    share = coupling_ref[...] / diagonal
     blank = jnp.zeros((6, 64), F32)
-    static[0:6, :] = jnp.concatenate([share, blank], axis=1)
+    static[0:6, :] = jnp.concatenate([coupling_ref[...] / diagonal, blank], axis=1)
     static[8:14, :] = jnp.concatenate([edges_ref[...].astype(F32), blank], axis=1)
-    static[16:24, :] = first_ref[...]
-    for c in range(3):
-        face_out[0, c] = faces_ref[c, pl.ds(7, 32, stride=8), :]
-        face_out[1, c] = faces_ref[c, pl.ds(0, 32, stride=8), :]
-
-    def place(state):
-        state = jnp.where(own_half, state, 0.0)
-        return jnp.where(g % 2 == 1, pltpu.roll(state, 64, axis=1), state)[0:4, :]
-
-    near[0, g] = place(first_ref[...])
     pl.semaphore_wait(barrier, GROUPS - 1 + SPANS - 1)
 
-    def push_near(r):
-        def push(k, carry):
-            peer = (g + k) % GROUPS
-            pltpu.make_async_remote_copy(
-                near.at[r, g], near.at[r, g], near_send.at[r], near_recv.at[r],
-                device_id=(peer, s), device_id_type=MESH,
-            ).start()
-            return carry
-
-        lax.fori_loop(1, GROUPS, push, 0)
-
-    push_near(0)
-    up, down = (s + 1) % SPANS, (s + SPANS - 1) % SPANS
+    def push_send(k, carry):
+        peer = offset_peer(g, k)
+        pltpu.make_async_remote_copy(
+            send.at[peer], recv.at[g], send_sem, recv_sem.at[g], device_id=(peer, s), device_id_type=MESH
+        ).start()
+        return carry
+
+    lax.fori_loop(0, GROUPS - 1, push_send, 0)
     halos = [
         pltpu.make_async_remote_copy(
             src, dst, halo_send.at[n], halo_recv.at[n], device_id=(g, to), device_id_type=MESH
         )
         for n, (src, dst, to) in enumerate(
             [
-                (static, low_in, up),
-                (static, high_in, down),
-                (face_out.at[0], low_ref, up),
-                (face_out.at[1], high_ref, down),
+                (static, low_in, up), (static, high_in, down),
+                (first_ref, first_low, up), (first_ref, first_high, down),
+                (face_out.at[0], low_ref, up), (face_out.at[1], high_ref, down),
             ]
         )
     ]
-    for halo in halos:
-        halo.start()
+    halos[0].start()
+    halos[1].start()
+    total[...] = add_up(recv, [g])
     halos[0].wait_recv()
     halos[1].wait_recv()
-    turn = lane & 7
-
-    def extended(rows):
-        beyond = jnp.where(turn == 7, low_in[rows, :], jnp.where(turn == 0, high_in[rows, :], 0.0))
-        return jnp.where(own_half, static[rows, :], pltpu.roll(beyond, 64, axis=1))
-
-    share = extended(slice(0, 8))
-    edges = extended(slice(8, 16)).astype(I32)
-    first = extended(slice(16, 24))
+    lane = iota((8, 128), 1)
+    own_half, turn = lane < 64, lane & 7
+
+    def extended(own, below, above):
+        beyond = jnp.where(turn == 7, below, jnp.where(turn == 0, above, 0.0))
+        return jnp.where(own_half, own, pltpu.roll(beyond, 64, axis=1))
+
+    share, edges = [
+        extended(static[rows, :], low_in[rows, :], high_in[rows, :]) for rows in (slice(0, 8), slice(8, 16))
+    ]
+    edges = edges.astype(I32)
     for d in range(6):
         node = edges[d : d + 1, :]
         group, span, local = node >> 9, (node >> 6) & 7, node & 63
@@ -276,7 +197,54 @@
         picks[128:256, cols] = pick
         line = span * 16 + (group >> 1)
         weights[:, cols] = jnp.where(iota((128, 128), 0) == line, share[d : d + 1, :], 0.0)
+
+    for k in range(GROUPS - 2, -1, -TOGETHER):
+        sources = [offset_peer(g, n) for n in range(k, max(k - TOGETHER, -1), -1)]
+        for source in sources:
+            wait_for(recv.at[source], recv_sem.at[source])
+        total[...] += add_up(recv, sources)
+
     row = iota((8, 128), 0)
+    first = jnp.zeros((8, 128), F32)
+    for c in range(3):
+        sums = total[2 * c * NP : (2 * c + 1) * NP, :] + total[(2 * c + 1) * NP : (2 * c + 2) * NP, :]
+        load = jnp.sum(sums, axis=0, keepdims=True)
+        load = load[:, 0:128] + load[:, 128:256]
+        load = load + pltpu.roll(load, 64, axis=1)
+        value = (force_ref[c : c + 1, :] + 0.25 * load[:, 0:64]) / diagonal
+        first = jnp.where(row == c, jnp.concatenate([value, value], axis=1), first)
+        total[2 * c * NP : (2 * c + 1) * NP, :] = sums
+    first_ref[...] = first
+
+    def place(state):
+        state = jnp.where(own_half, state, 0.0)
+        return jnp.where(g % 2 == 1, pltpu.roll(state, 64, axis=1), state)[0:4, :]
+
+    def push_near(r):
+        def push(k, carry):
+            pltpu.make_async_remote_copy(
+                near.at[r, g], near.at[r, g], near_send.at[r], near_recv.at[r],
+                device_id=(offset_peer(g, k), s), device_id_type=MESH,
+            ).start()
+            return carry
+
+        lax.fori_loop(0, GROUPS - 1, push, 0)
+
+    near[0, g] = place(first)
+    push_near(0)
+    halos[2].start()
+    halos[3].start()
+    for c in range(3):
+        full = jnp.concatenate([total[2 * c * NP : (2 * c + 1) * NP, :], jnp.zeros((128 - NP, 256), F32)], axis=0)
+        faces_ref[c] = full.T
+    for c in range(3):
+        face_out[0, c] = faces_ref[c, pl.ds(7, 32, stride=8), :]
+        face_out[1, c] = faces_ref[c, pl.ds(0, 32, stride=8), :]
+    halos[4].start()
+    halos[5].start()
+    halos[2].wait_recv()
+    halos[3].wait_recv()
+    first = extended(first, first_low[...], first_high[...])
     state = first
     for r in range(ROUNDS):
         wait_for(near.at[r, pl.ds(0, GROUPS - 1)], near_recv.at[r])
@@ -301,15 +269,16 @@
         weighted = weights[...].reshape(SPANS, 16, 768)
         state = first
         for c in range(3):
-            total = jnp.sum((found[:, c] * weighted).reshape(SPANS * 16, 768), axis=0, keepdims=True)
-            parts = [total[:, d * 128 : (d + 1) * 128] for d in range(6)]
+            sums = jnp.sum((found[:, c] * weighted).reshape(SPANS * 16, 768), axis=0, keepdims=True)
+            parts = [sums[:, d * 128 : (d + 1) * 128] for d in range(6)]
             state = state + jnp.where(row == c, functools.reduce(jnp.add, parts), 0.0)
         if r + 1 < ROUNDS:
             near[r + 1, g] = place(state)
             push_near(r + 1)
     skel_ref[...] = state
-    halos[2].wait_recv()
-    halos[3].wait_recv()
+    halos[4].wait_recv()
+    halos[5].wait_recv()
+    wait_for(send.at[pl.ds(0, GROUPS - 1)], send_sem)
     for halo in halos:
         halo.wait_send()
     for r in range(ROUNDS):
@@ -317,33 +286,39 @@
         wait_for(far.at[r, pl.ds(0, SPANS - 1)], far_send.at[r])
 
 
-def sweeps(first, coupling, stiff, edges, faces):
+def front(disp, weight, owner, row, force, coupling, stiff, edges):
     dma = pltpu.SemaphoreType.DMA
+    local = [pltpu.VMEM(x.shape, x.dtype) for x in (disp, weight, owner, row, force, coupling, stiff, edges)]
     return pl.pallas_call(
-        sweep_body,
-        name="sweeps",
+        front_body,
+        name="front",
         out_shape=(
+            jax.ShapeDtypeStruct((3, 256, 128), F32),
             jax.ShapeDtypeStruct((8, 128), F32),
             jax.ShapeDtypeStruct((3, 32, 128), F32),
             jax.ShapeDtypeStruct((3, 32, 128), F32),
         ),
-        in_specs=[VMEM_SPEC] * 5,
-        out_specs=(VMEM_SPEC,) * 3,
+        in_specs=[pl.BlockSpec(memory_space=pltpu.HBM)] * 8,
+        out_specs=(VMEM_SPEC,) * 4,
         scratch_shapes=[
-            pltpu.VMEM((24, 128), F32),
-            pltpu.VMEM((24, 128), F32),
-            pltpu.VMEM((24, 128), F32),
+            *local,
+            pltpu.VMEM((512, NODES), BF16), pltpu.VMEM((256, NODES), BF16),
+            pltpu.VMEM((GROUPS, 8, 256), F32), pltpu.VMEM((GROUPS, 8, 256), F32),
+            pltpu.VMEM((6 * NP, 256), F32),
+            pltpu.VMEM((8, 128), F32), pltpu.VMEM((8, 128), F32), pltpu.VMEM((8, 128), F32),
+            pltpu.VMEM((16, 128), F32), pltpu.VMEM((16, 128), F32), pltpu.VMEM((16, 128), F32),
             pltpu.VMEM((2, 3, 32, 128), F32),
             pltpu.VMEM((ROUNDS, GROUPS, 4, 128), F32),
             pltpu.VMEM((ROUNDS, SPANS, 48, 128), F32),
             pltpu.VMEM((256, 768), BF16),
             pltpu.VMEM((128, 768), F32),
-            dma((ROUNDS,)), dma((ROUNDS,)), dma((ROUNDS,)), dma((ROUNDS,)), dma((4,)), dma((4,)),
+            dma((8,)), dma, dma((GROUPS,)),
+            dma((ROUNDS,)), dma((ROUNDS,)), dma((ROUNDS,)), dma((ROUNDS,)), dma((6,)), dma((6,)),
         ],
         compiler_params=pltpu.CompilerParams(
-            collective_id=1, has_side_effects=True, vmem_limit_bytes=48 << 20
-        ),
-    )(first, coupling, stiff, edges, faces)
+            collective_id=0, has_side_effects=True, vmem_limit_bytes=48 << 20
+        ),
+    )(disp, weight, owner, row, force, coupling, stiff, edges)
 
 
 def blend_tables():
@@ -478,11 +453,9 @@
 
 
 def on_device(disp, weight, owner, row, force, coupling, stiff, edges, spacing):
-    stiff = stiff.reshape(1, -1)
-    send = pack(disp, weight.T, owner.T, row.T)
-    recv = exchange(send)
-    faces, first = add_up(recv, force, coupling, stiff)
-    skel, low, high = sweeps(first, coupling, stiff, edges, faces)
+    faces, skel, low, high = front(
+        disp, weight.T, owner.T, row.T, force, coupling, stiff.reshape(1, -1), edges
+    )
     return blend(spacing, faces, low, high, skel)
 
 

time: 98.6 us -> 86.4 us (0.88)
  Pallas kernels: 87.4 us -> 76.9 us
  local copies, waits for them, and re-layouts: 9.9 us -> 8.27 us
    pallas_call x4 -> x1, Pallas kernels: 73.1 us -> 62.6 us  [front(): pl.pallas_call(front_body, name='front', out_shape=(jax.ShapeDtypeStruct(...]
    unnamed x26 -> x22, local copies, waits for them, and re-layouts: 9.9 us -> 8.27 us
where the time goes in v2:
time: 86.4 us; the launch traced here: 85.9 us
  Pallas kernels  76.9 us (89%)
  local copies, waits for them, and re-layouts  8.27 us (10%)
    pallas_call x1, Pallas kernels, front(): pl.pallas_call(front_body, name='front', out_shape=(jax.ShapeDtypeStruct(...  62.6 us
    pallas_call x1, Pallas kernels, blend(): pl.pallas_call(blend_body, name='blend', grid=(8,), out_shape=(jax.ShapeD...  14.3 us
    unnamed x22, local copies, waits for them, and re-layouts  8.27 us

profile of v2, /device:TPU:1, one launch (start us, length us, event | category | flops | bytes accessed | tf_op | source)
XLA Modules:
  0.0 85.9 jit_solution(14065272524605689957)
XLA Ops:
  0.6 0.0 copy-start.2
  0.6 0.7 copy-done.2
  1.4 0.0 copy-start.3
  1.4 0.8 copy-done.3
  2.1 0.0 copy-start.4
  2.2 0.8 copy-done.4
  2.9 0.0 copy-start.5
  2.9 0.8 copy-done.5
  3.7 0.0 copy-start.6
  3.7 0.7 copy-done.6
  4.4 0.0 copy-start.7
  4.4 0.7 copy-done.7
  5.0 0.0 copy-start.8
  5.0 0.7 copy-done.8
  5.7 0.0 copy-start.10
  5.7 0.7 copy-done.10
  6.4 62.6 %front.1 = (f32[3,256,128]{2,1,0:T(8,128)S(1)}, f32[8,128]{1,0:T(8,128)S(1)}, f32[3,32,128]{2,1,0:T(8,128)S(1)}, f32[3,32,128]{2,1,0:T(8,128)S(1)}) custom-call(f32[3,2048]{1,0:T(4,128)S(1)} %copy-done.2, f32[4,2048]{1,0:T(4,128)S(1)} %bitcast.4, s32[4,2048]{1,0:T(4,128)S(1)} %bitcast.5, s32[4,2048]{1,0:T(4,128)S(1)} %bitcast.6, f32[3,64]{1,0:T(4,128)S(1)} %copy-done.8, ...), custom_call_target="tpu_custom_call" | custom-call | tf_op jit(solution)/shard_map/front/pallas_call | solution.py:292
  69.0 0.0 copy-start
  69.0 0.9 %copy-done = s32[8,6400]{1,0:T(8,128)S(1)} copy-done((s32[8,6400]{1,0:T(8,128)S(1)}, s32[8,6400]{1,0:T(8,128)}, u32[]{:S(2)}) %copy-start) | copy-done | bytes 204824
  69.9 0.0 copy-start.1
  69.9 0.9 %copy-done.1 = f32[8,6400]{1,0:T(8,128)S(1)} copy-done((f32[8,6400]{1,0:T(8,128)S(1)}, f32[8,6400]{1,0:T(8,128)}, u32[]{:S(2)}) %copy-start.1) | copy-done | bytes 204824
  70.8 0.0 copy-start.9
  70.8 0.7 copy-done.9
  71.5 14.3 %blend.1 = (f32[3,8,8,6400]{3,2,1,0:T(8,128)}, f32[8,8,6400]{2,1,0:T(8,128)}) custom-call(f32[3,8]{1,0:T(4,128)S(1)} %copy-done.9, f32[3,256,128]{2,1,0:T(8,128)S(1)} %get-tuple-element.6.faces_ref, f32[3,32,128]{2,1,0:T(8,128)S(1)} %get-tuple-element.7.low_ref, f32[3,32,128]{2,1,0:T(8,128)S(1)} %get-tuple-element.8.high_ref, ...), custom_call_target="tpu_custom_call" | custom-call | tf_op jit(solution)/shard_map/blend/pallas_call | solution.py:428
Async XLA Ops:
  0.6 0.8 copy-start.2
  1.4 0.8 copy-start.3
  2.1 0.8 copy-start.4
  2.9 0.8 copy-start.5
  3.7 0.7 copy-start.6
  4.4 0.7 copy-start.7
  5.0 0.7 copy-start.8
  5.7 0.7 copy-start.10
  69.0 0.9 %copy-start = (s32[8,6400]{1,0:T(8,128)S(1)}, s32[8,6400]{1,0:T(8,128)}, u32[]{:S(2)}) copy-start(s32[8,6400]{1,0:T(8,128)} %constant.5.clone.index_ref) | copy-start | bytes 614404
  69.9 0.9 %copy-start.1 = (f32[8,6400]{1,0:T(8,128)S(1)}, f32[8,6400]{1,0:T(8,128)}, u32[]{:S(2)}) copy-start(f32[8,6400]{1,0:T(8,128)} %constant.4.clone.table_ref) | copy-start | bytes 614404
  70.8 0.7 copy-start.9

commit v3 on v2

--- a/solution.py
+++ b/solution.py
@@ -104,7 +104,7 @@
     )
 
 
-ROUNDS = 3
+ROUNDS = 2
 TOGETHER = 4
 
 
@@ -112,9 +112,10 @@
     disp_hbm, weight_hbm, owner_hbm, row_hbm, force_hbm, coupling_hbm, stiff_hbm, edges_hbm,
     faces_ref, skel_ref, low_ref, high_ref,
     disp_ref, weight_ref, owner_ref, row_ref, force_ref, coupling_ref, stiff_ref, edges_ref,
-    lhs, rhs, send, recv, total, first_ref, first_low, first_high,
-    static, low_in, high_in, face_out, near, far, picks, weights,
+    lhs, rhs, send, recv, total,
+    static, low_in, high_in, face_out, near, far, picks, weights, near_rows, far_rows, picks2, weights2,
     load_sem, send_sem, recv_sem, near_send, near_recv, far_send, far_recv, halo_send, halo_recv,
+    rows_send, rows_recv,
 ):
     g, s = lax.axis_index("group"), lax.axis_index("span")
     up, down = (s + 1) % SPANS, (s + SPANS - 1) % SPANS
@@ -149,6 +150,13 @@
     blank = jnp.zeros((6, 64), F32)
     static[0:6, :] = jnp.concatenate([coupling_ref[...] / diagonal, blank], axis=1)
     static[8:14, :] = jnp.concatenate([edges_ref[...].astype(F32), blank], axis=1)
+    near_rows[g] = jnp.concatenate(
+        [
+            jnp.concatenate([coupling_ref[...] / diagonal, edges_ref[...].astype(F32)], axis=1),
+            jnp.zeros((2, 128), F32),
+        ],
+        axis=0,
+    )
     pl.semaphore_wait(barrier, GROUPS - 1 + SPANS - 1)
 
     def push_send(k, carry):
@@ -166,13 +174,21 @@
         for n, (src, dst, to) in enumerate(
             [
                 (static, low_in, up), (static, high_in, down),
-                (first_ref, first_low, up), (first_ref, first_high, down),
                 (face_out.at[0], low_ref, up), (face_out.at[1], high_ref, down),
             ]
         )
     ]
     halos[0].start()
     halos[1].start()
+
+    def push_near_rows(k, carry):
+        pltpu.make_async_remote_copy(
+            near_rows.at[g], near_rows.at[g], rows_send.at[0], rows_recv.at[0],
+            device_id=(offset_peer(g, k), s), device_id_type=MESH,
+        ).start()
+        return carry
+
+    lax.fori_loop(0, GROUPS - 1, push_near_rows, 0)
     total[...] = add_up(recv, [g])
     halos[0].wait_recv()
     halos[1].wait_recv()
@@ -187,19 +203,41 @@
         extended(static[rows, :], low_in[rows, :], high_in[rows, :]) for rows in (slice(0, 8), slice(8, 16))
     ]
     edges = edges.astype(I32)
-    for d in range(6):
-        node = edges[d : d + 1, :]
+    sublane = iota((128, 128), 0)
+
+    def locate(node):
         group, span, local = node >> 9, (node >> 6) & 7, node & 63
-        column = (group & 1) * 64 + local
-        pick = jnp.where(iota((128, 128), 0) == column, 1.0, 0.0).astype(BF16)
+        return span * 16 + (group >> 1), (group & 1) * 64 + local
+
+    here = iota((1, 128), 1)
+    below = (g * SPANS + down) * 64 + here - 64
+    above = (g * SPANS + up) * 64 + here - 64
+    itself = jnp.where(here < 64, (g * SPANS + s) * 64 + here, jnp.where((here & 7) == 7, below, above))
+    for d in range(7):
+        line, column = locate(edges[d : d + 1, :] if d < 6 else itself)
         cols = slice(d * 128, (d + 1) * 128)
-        picks[0:128, cols] = pick
-        picks[128:256, cols] = pick
-        line = span * 16 + (group >> 1)
-        weights[:, cols] = jnp.where(iota((128, 128), 0) == line, share[d : d + 1, :], 0.0)
-
-    for k in range(GROUPS - 2, -1, -TOGETHER):
-        sources = [offset_peer(g, n) for n in range(k, max(k - TOGETHER, -1), -1)]
+        picks[:, cols] = jnp.where(sublane == column, 1.0, 0.0).astype(BF16)
+        weights[:, cols] = jnp.where(sublane == line, share[d : d + 1, :] if d < 6 else 1.0, 0.0)
+
+    wait_for(near_rows.at[pl.ds(0, GROUPS - 1)], rows_recv.at[0])
+    for h in range(16):
+        even, odd = near_rows[2 * h], near_rows[2 * h + 1]
+        pair = jnp.where(own_half, even, pltpu.roll(odd, 64, axis=1))
+        ends = jnp.where(own_half, pltpu.roll(even, 64, axis=1), odd)
+        for d in range(6):
+            far_rows[s, d * 16 + h : d * 16 + h + 1, :] = pair[d : d + 1, :]
+            far_rows[s, 96 + d * 16 + h : 96 + d * 16 + h + 1, :] = ends[d : d + 1, :]
+
+    def push_far_rows(k, carry):
+        pltpu.make_async_remote_copy(
+            far_rows.at[s], far_rows.at[s], rows_send.at[1], rows_recv.at[1],
+            device_id=(g, (s + k) % SPANS), device_id_type=MESH,
+        ).start()
+        return carry
+
+    lax.fori_loop(1, SPANS, push_far_rows, 0)
+    for k in range(0, GROUPS - 1, TOGETHER):
+        sources = [offset_peer(g, n) for n in range(k, min(k + TOGETHER, GROUPS - 1))]
         for source in sources:
             wait_for(recv.at[source], recv_sem.at[source])
         total[...] += add_up(recv, sources)
@@ -214,8 +252,6 @@
         value = (force_ref[c : c + 1, :] + 0.25 * load[:, 0:64]) / diagonal
         first = jnp.where(row == c, jnp.concatenate([value, value], axis=1), first)
         total[2 * c * NP : (2 * c + 1) * NP, :] = sums
-    first_ref[...] = first
-
     def place(state):
         state = jnp.where(own_half, state, 0.0)
         return jnp.where(g % 2 == 1, pltpu.roll(state, 64, axis=1), state)[0:4, :]
@@ -232,20 +268,47 @@
 
     near[0, g] = place(first)
     push_near(0)
-    halos[2].start()
-    halos[3].start()
     for c in range(3):
         full = jnp.concatenate([total[2 * c * NP : (2 * c + 1) * NP, :], jnp.zeros((128 - NP, 256), F32)], axis=0)
         faces_ref[c] = full.T
     for c in range(3):
         face_out[0, c] = faces_ref[c, pl.ds(7, 32, stride=8), :]
         face_out[1, c] = faces_ref[c, pl.ds(0, 32, stride=8), :]
-    halos[4].start()
-    halos[5].start()
-    halos[2].wait_recv()
-    halos[3].wait_recv()
-    first = extended(first, first_low[...], first_high[...])
-    state = first
+    halos[2].start()
+    halos[3].start()
+    wait_for(far_rows.at[pl.ds(0, SPANS - 1)], rows_recv.at[1])
+    links = [static[8 + d : 9 + d, :].astype(I32) for d in range(6)]
+    joint = [jnp.where(here < 64, links[2 * t], pltpu.roll(links[2 * t + 1], 64, axis=1)) for t in range(3)]
+    parts = [static[d : d + 1, :] for d in range(6)]
+    shares = [jnp.where(here < 64, parts[2 * t], pltpu.roll(parts[2 * t + 1], 64, axis=1)) for t in range(3)]
+    rows_table = jnp.concatenate(split(far_rows[...].reshape(SPANS * 192, 128)), axis=1)
+    for t in range(3):
+        line, column = locate(joint[t])
+        pick = jnp.where(sublane == column, 1.0, 0.0).astype(BF16)
+        found = jnp.dot(rows_table, jnp.concatenate([pick, pick], axis=0), preferred_element_type=F32)
+        found = found.reshape(SPANS, 12, 16, 128)
+        mask = jnp.where(sublane == line, 1.0, 0.0).reshape(SPANS, 16, 128)
+        for d in range(6):
+            share2 = jnp.sum((found[:, d] * mask).reshape(128, 128), axis=0, keepdims=True)
+            link2 = jnp.sum((found[:, 6 + d] * mask).reshape(128, 128), axis=0, keepdims=True)
+            line2, column2 = locate(link2.astype(I32))
+            cols = slice((t * 6 + d) * 128, (t * 6 + d + 1) * 128)
+            picks2[:, cols] = jnp.where(sublane == column2, 1.0, 0.0).astype(BF16)
+            weights2[:, cols] = jnp.where(sublane == line2, share2 * shares[t], 0.0)
+
+    def combine(table, pick, weight):
+        table = jnp.concatenate(split(table), axis=1)
+        out = jnp.zeros((8, 128), F32)
+        found = jnp.dot(table, jnp.concatenate([pick, pick], axis=0), preferred_element_type=F32)
+        width = pick.shape[1]
+        found = found.reshape(SPANS, 3, 16, width)
+        weighted = weight.reshape(SPANS, 16, width)
+        for c in range(3):
+            sums = jnp.sum((found[:, c] * weighted).reshape(SPANS * 16, width), axis=0, keepdims=True)
+            parts = [sums[:, d * 128 : (d + 1) * 128] for d in range(width // 128)]
+            out = jnp.where(row == c, functools.reduce(jnp.add, parts), out)
+        return out
+
     for r in range(ROUNDS):
         wait_for(near.at[r, pl.ds(0, GROUPS - 1)], near_recv.at[r])
         for h in range(16):
@@ -264,23 +327,20 @@
         lax.fori_loop(1, SPANS, push, 0)
         wait_for(far.at[r, pl.ds(0, SPANS - 1)], far_recv.at[r])
         table = far[r].reshape(SPANS * 48, 128)
-        found = jnp.dot(jnp.concatenate(split(table), axis=1), picks[...], preferred_element_type=F32)
-        found = found.reshape(SPANS, 3, 16, 768)
-        weighted = weights[...].reshape(SPANS, 16, 768)
-        state = first
-        for c in range(3):
-            sums = jnp.sum((found[:, c] * weighted).reshape(SPANS * 16, 768), axis=0, keepdims=True)
-            parts = [sums[:, d * 128 : (d + 1) * 128] for d in range(6)]
-            state = state + jnp.where(row == c, functools.reduce(jnp.add, parts), 0.0)
-        if r + 1 < ROUNDS:
-            near[r + 1, g] = place(state)
-            push_near(r + 1)
+        if r == 0:
+            sums = combine(table, picks2[...], weights2[...])
+            near[1, g] = place(first + sums + pltpu.roll(sums, 64, axis=1))
+            push_near(1)
+        else:
+            state = combine(table, picks[...], weights[...])
     skel_ref[...] = state
-    halos[4].wait_recv()
-    halos[5].wait_recv()
+    halos[2].wait_recv()
+    halos[3].wait_recv()
     wait_for(send.at[pl.ds(0, GROUPS - 1)], send_sem)
     for halo in halos:
         halo.wait_send()
+    wait_for(near_rows.at[pl.ds(0, GROUPS - 1)], rows_send.at[0])
+    wait_for(far_rows.at[pl.ds(0, SPANS - 1)], rows_send.at[1])
     for r in range(ROUNDS):
         wait_for(near.at[r, pl.ds(0, GROUPS - 1)], near_send.at[r])
         wait_for(far.at[r, pl.ds(0, SPANS - 1)], far_send.at[r])
@@ -305,27 +365,32 @@
             pltpu.VMEM((512, NODES), BF16), pltpu.VMEM((256, NODES), BF16),
             pltpu.VMEM((GROUPS, 8, 256), F32), pltpu.VMEM((GROUPS, 8, 256), F32),
             pltpu.VMEM((6 * NP, 256), F32),
-            pltpu.VMEM((8, 128), F32), pltpu.VMEM((8, 128), F32), pltpu.VMEM((8, 128), F32),
             pltpu.VMEM((16, 128), F32), pltpu.VMEM((16, 128), F32), pltpu.VMEM((16, 128), F32),
             pltpu.VMEM((2, 3, 32, 128), F32),
             pltpu.VMEM((ROUNDS, GROUPS, 4, 128), F32),
             pltpu.VMEM((ROUNDS, SPANS, 48, 128), F32),
-            pltpu.VMEM((256, 768), BF16),
-            pltpu.VMEM((128, 768), F32),
+            pltpu.VMEM((128, 896), BF16), pltpu.VMEM((128, 896), F32),
+            pltpu.VMEM((GROUPS, 8, 128), F32), pltpu.VMEM((SPANS, 192, 128), F32),
+            pltpu.VMEM((128, 2304), BF16), pltpu.VMEM((128, 2304), F32),
             dma((8,)), dma, dma((GROUPS,)),
-            dma((ROUNDS,)), dma((ROUNDS,)), dma((ROUNDS,)), dma((ROUNDS,)), dma((6,)), dma((6,)),
+            dma((ROUNDS,)), dma((ROUNDS,)), dma((ROUNDS,)), dma((ROUNDS,)), dma((4,)), dma((4,)),
+            dma((2,)), dma((2,)),
         ],
         compiler_params=pltpu.CompilerParams(
-            collective_id=0, has_side_effects=True, vmem_limit_bytes=48 << 20
+            collective_id=0, has_side_effects=True, vmem_limit_bytes=63 << 20
         ),
     )(disp, weight, owner, row, force, coupling, stiff, edges)
 
 
-def blend_tables():
+HALF = NP * NP // 2
+CHUNK = 640
+CHUNKS = NP * NP // CHUNK
+
+
+def blend_table():
     f = np.arange(NP * NP)
     i, j = f % NP, f // NP
     n = NP - 1
-    s, t = i / n, j / n
 
     def bubble(i, j):
         s, t = i / n, j / n
@@ -333,29 +398,35 @@
 
     ip, im = np.minimum(i + 1, n), np.maximum(i - 1, 0)
     jp, jm = np.minimum(j + 1, n), np.maximum(j - 1, 0)
-    rows = [
-        s, t, (ip - im) / (2.0 * n), (jp - jm) / (2.0 * n),
-        bubble(i, j), 0.5 * (bubble(ip, j) - bubble(im, j)), 0.5 * (bubble(i, jp) - bubble(i, jm)),
-    ]
-    rows.append(np.zeros_like(s))
-    return np.stack(rows).astype(np.float32), np.stack([i, j] + [i] * 6).astype(np.int32)
-
-
-def pick_lanes(x, index):
-    return jnp.take_along_axis(x, index, axis=1)
-
-
-def blend_body(spacing_ref, faces_ref, low_ref, high_ref, skel_ref, table_ref, index_ref, disp_ref, jac_ref):
-    q = pl.program_id(0)
+    hit = (j[None] % 40 == np.arange(40)[:, None]).astype(np.float64)
+    rows = [hit, hit * i, hit * (ip - im)]
+    for bump in (
+        bubble(i, j), 0.5 * (bubble(ip, j) - bubble(im, j)), 0.5 * (bubble(i, jp) - bubble(i, jm))
+    ):
+        high = bump.astype(BF16).astype(np.float64)
+        rows += [high[None], (bump - high)[None]]
+    rows.append(np.zeros((2, NP * NP)))
+    return np.concatenate(rows).astype(BF16)
+
+
+def column_of(values):
+    return jnp.concatenate([jnp.full((8, 128), value, F32) for value in values], axis=0)
+
+
+def prepare(faces_ref, low_ref, high_ref, spacing_ref, lhs_ref, fns_ref):
     span = lax.axis_index("span")
     has_low = jnp.where(span > 0, 1.0, 0.0).astype(F32)
     has_high = jnp.where(span < SPANS - 1, 1.0, 0.0).astype(F32)
-    row, lane = iota((8, 128), 0), iota((8, 128), 1)
+    lane = iota((LAYERS, 128), 1)
+    turn = iota((LAYERS, 128), 0) & 7
     frac = lane.astype(F32) * (1.0 / (NP - 1))
 
-    def along_span(x, before, after):
-        nxt = jnp.where(row == 7, after * has_high, pltpu.roll(x, 7, axis=0))
-        prv = jnp.where(row == 0, before * has_low, pltpu.roll(x, 1, axis=0))
+    def along_span(x, c, seg):
+        rows = [slice(seg * 8 + q, seg * 8 + q + 1) for q in range(8)]
+        before = jnp.concatenate([jnp.broadcast_to(low_ref[c, r, :], (8, 128)) for r in rows], axis=0)
+        after = jnp.concatenate([jnp.broadcast_to(high_ref[c, r, :], (8, 128)) for r in rows], axis=0)
+        nxt = jnp.where(turn == 7, after * has_high, pltpu.roll(x, LAYERS - 1, axis=0))
+        prv = jnp.where(turn == 0, before * has_low, pltpu.roll(x, 1, axis=0))
         return 0.5 * (nxt - prv)
 
     def along_lane(x):
@@ -366,90 +437,181 @@
     def inner(x):
         return x - (1.0 - frac) * x[:, 0:1] - frac * x[:, NP - 1 : NP]
 
-    lane_fns, column_fns, bumps = [], [], []
     for c in range(3):
-        now, diff = [], []
-        for seg in range(4):
-            x = faces_ref[c, pl.ds(pl.multiple_of(seg * LAYERS + q * 8, 8), 8), :]
-            before = low_ref[c, pl.ds(seg * 8 + q, 1), :]
-            after = high_ref[c, pl.ds(seg * 8 + q, 1), :]
-            now.append(x)
-            diff.append(along_span(x, before, after))
+        now = [faces_ref[c, seg * LAYERS : (seg + 1) * LAYERS, :] for seg in range(4)]
+        diff = [along_span(x, c, seg) for seg, x in enumerate(now)]
         values = []
         for bottom, top, left, right in (now, diff):
             base = inner(bottom)
-            values.append((base, inner(top) - base, left, right - left))
+            values.append((base, inner(top) - base, left, (right - left) * (1.0 / (NP - 1))))
         (b, d, left, m), (b_s, d_s, left_s, m_s) = values
-        lane_fns.append((b, d, along_lane(b), along_lane(d), b_s, d_s))
-        column_fns.append((left, m, along_lane(left), along_lane(m), left_s, m_s))
-        skel = jnp.broadcast_to(skel_ref[c : c + 1, :], (8, 128))
+        b_i, left_j = along_lane(b), along_lane(left)
+        if c == 0:
+            b_i = b_i + column_of([spacing_ref[c, q] for q in range(8)])
+        elif c == 1:
+            left_j = left_j + column_of([spacing_ref[c, q] for q in range(8)])
+        else:
+            b_s = b_s + column_of([spacing_ref[c, q] for q in range(8)])
+        for n, fn in enumerate((b, d, b_i, along_lane(d), b_s, d_s)):
+            for phase in range(5):
+                at = lane[0:8] + (phase * 128) % NP
+                at = jnp.where(at >= NP, at - NP, at)
+                at = jnp.where(at >= NP, at - NP, at)
+                for q in range(8):
+                    rows = slice(q * 8, q * 8 + 8)
+                    fns_ref[phase, n, c, rows, :] = jnp.take_along_axis(fn[rows], at, axis=1)
+        for half in range(2):
+            shift = (128 - 40 * half) % 128
+            fields = [None] * 4
+            for n, (x, y) in ((0, (left, m)), (2, (left_j, along_lane(m))), (3, (left_s, m_s))):
+                x = pltpu.roll(x, shift, axis=1) if half else x
+                y = y if half else pltpu.roll(y, 40, axis=1)
+                fields[n] = jnp.where(lane < 40, x, jnp.where(lane < 80, y, 0.0))
+            x = pltpu.roll(0.5 * m, 40 if half else 80, axis=1)
+            fields[1] = jnp.where((lane >= 80) & (lane < 120), x, 0.0)
+            for n, field in enumerate(fields):
+                high, low = split(field)
+                rows = slice((n * 3 + c) * LAYERS, (n * 3 + c + 1) * LAYERS)
+                lhs_ref[half, rows, 0:128] = high
+                lhs_ref[half, rows, 128:256] = low
+
+
+def place_bumps(skel_ref, lhs_ref):
+    span = lax.axis_index("span")
+    has_low = jnp.where(span > 0, 1.0, 0.0).astype(F32)
+    has_high = jnp.where(span < SPANS - 1, 1.0, 0.0).astype(F32)
+    lane, row = iota((LAYERS, 128), 1), iota((LAYERS, 128), 0)
+    turn = row & 7
+    for c in range(3):
+        skel = jnp.broadcast_to(skel_ref[c : c + 1, :], (LAYERS, 128))
 
         def column(where):
             return jnp.sum(jnp.where(where, skel, 0.0), axis=1, keepdims=True)
 
-        value = column(lane == q * 8 + row)
-        nxt = column(lane == jnp.where(row == 7, 64 + q * 8, q * 8 + row + 1))
-        prv = column(lane == jnp.where(row == 0, 64 + q * 8 + 7, q * 8 + row - 1))
-        nxt = jnp.where(row == 7, nxt * has_high, nxt)
-        prv = jnp.where(row == 0, prv * has_low, prv)
-        bumps.append((jnp.broadcast_to(value, (8, 128)), 0.5 * (nxt - prv)))
-    spacing = [spacing_ref[c, q] for c in range(3)]
-
-    for phase in range(5):
-        where = jnp.broadcast_to(index_ref[0:1, phase * 128 : (phase + 1) * 128], (8, 128))
-        lanes = [[pick_lanes(x, where) for x in fns] for fns in lane_fns]
-        for turn in range(10):
-            cols = slice((turn * 5 + phase) * 128, (turn * 5 + phase + 1) * 128)
-            where = jnp.broadcast_to(index_ref[1:2, cols], (8, 128))
-            s, t, s_i, t_j, bump, bump_i, bump_j = [table_ref[n : n + 1, cols] for n in range(7)]
-            matrix = []
-            for c in range(3):
-                b, d, b_i, d_i, b_s, d_s = lanes[c]
-                left, m, left_j, m_j, left_s, m_s = [pick_lanes(x, where) for x in column_fns[c]]
-                k, k_s = bumps[c]
-                disp_ref[c, 0, :, cols] = b + t * d + left + s * m + bump * k
-                matrix.append(
-                    [
-                        b_i + t * d_i + s_i * m + bump_i * k,
-                        t_j * d + left_j + s * m_j + bump_j * k,
-                        b_s + t * d_s + left_s + s * m_s + bump * k_s,
+        value = column(lane == row)
+        nxt = column(lane == jnp.where(turn == 7, 64 + row - 7, row + 1))
+        prv = column(lane == jnp.where(turn == 0, 64 + row + 7, row - 1))
+        nxt = jnp.where(turn[:, 0:1] == 7, nxt * has_high, nxt)
+        prv = jnp.where(turn[:, 0:1] == 0, prv * has_low, prv)
+        diff = 0.5 * (nxt - prv)
+        for n, (x, first) in enumerate(((value, 120), (value, 122), (value, 124), (diff, 120))):
+            rows = slice((n * 3 + c) * LAYERS, (n * 3 + c + 1) * LAYERS)
+            mine = (lane == first) | (lane == first + 1)
+            for part, cols in zip(split(jnp.where(mine, x, 0.0)), (slice(0, 128), slice(128, 256))):
+                for half in range(2):
+                    lhs_ref[half, rows, cols] = lhs_ref[half, rows, cols] + part
+
+
+def blend_body(
+    spacing_ref, faces_hbm, low_hbm, high_hbm, skel_hbm, table_hbm, disp_hbm, jac_hbm,
+    faces_ref, low_ref, high_ref, skel_ref, table_ref, lhs_ref, fns_ref, even, odd, disp_ref, jac_ref,
+    load_sem, store_sem,
+):
+    loads = [
+        pltpu.make_async_copy(src, dst, load_sem.at[n])
+        for n, (src, dst) in enumerate(
+            [
+                (faces_hbm, faces_ref), (low_hbm, low_ref), (high_hbm, high_ref), (skel_hbm, skel_ref),
+                (table_hbm, table_ref),
+            ]
+        )
+    ]
+    for load in loads:
+        load.start()
+    for load in loads[:4]:
+        load.wait()
+    prepare(faces_ref, low_ref, high_ref, spacing_ref, lhs_ref, fns_ref)
+    place_bumps(skel_ref, lhs_ref)
+    loads[4].wait()
+
+    def cols_of(n):
+        return pl.ds(pl.multiple_of(n * CHUNK, 128), CHUNK)
+
+    def multiply(n, out):
+        table = table_ref[:, cols_of(n)]
+        out[...] = jnp.dot(
+            lhs_ref[n // (CHUNKS // 2)], jnp.concatenate([table, table], axis=0), preferred_element_type=F32
+        )
+
+    def finish(n, found):
+        place = iota((8, 128), 1)
+        for phase in range(5):
+            cols = slice(phase * 128, (phase + 1) * 128)
+            far = place + phase * 128
+            j = n * (CHUNK // NP) + sum(jnp.where(far >= NP * k, 1, 0) for k in range(1, CHUNK // NP))
+            t = j.astype(F32) * (1.0 / (NP - 1))
+            t_j = jnp.where((j == 0) | (j == NP - 1), 0.5 / (NP - 1), 1.0 / (NP - 1))
+            out_cols = pl.ds(pl.multiple_of(n * CHUNK + phase * 128, 128), 128)
+            for q in range(8):
+                matrix = []
+                for c in range(3):
+                    b, d, b_i, d_i, b_s, d_s = [
+                        fns_ref[phase, k, c, q * 8 : q * 8 + 8, :] for k in range(6)
                     ]
-                )
-                matrix[c][c] = matrix[c][c] + spacing[c]
-            one = matrix[1][1] * matrix[2][2] - matrix[1][2] * matrix[2][1]
-            two = matrix[1][0] * matrix[2][2] - matrix[1][2] * matrix[2][0]
-            three = matrix[1][0] * matrix[2][1] - matrix[1][1] * matrix[2][0]
-            jac_ref[0, :, cols] = matrix[0][0] * one - matrix[0][1] * two + matrix[0][2] * three
+                    x, x_i, x_j, x_s = [
+                        found[(k * 3 + c) * LAYERS + q * 8 : (k * 3 + c) * LAYERS + q * 8 + 8, cols]
+                        for k in range(4)
+                    ]
+                    disp_ref[c, q, :, out_cols] = x + b + t * d
+                    matrix.append([x_i + b_i + t * d_i, x_j + t_j * d, x_s + b_s + t * d_s])
+                one = matrix[1][1] * matrix[2][2] - matrix[1][2] * matrix[2][1]
+                two = matrix[1][0] * matrix[2][2] - matrix[1][2] * matrix[2][0]
+                three = matrix[1][0] * matrix[2][1] - matrix[1][1] * matrix[2][0]
+                jac_ref[q, :, out_cols] = matrix[0][0] * one - matrix[0][1] * two + matrix[0][2] * three
+
+    def stores(n):
+        cols = cols_of(n)
+        return (
+            pltpu.make_async_copy(disp_ref.at[:, :, :, cols], disp_hbm.at[:, :, :, cols], store_sem.at[0, n]),
+            pltpu.make_async_copy(jac_ref.at[:, :, cols], jac_hbm.at[:, :, cols], store_sem.at[1, n]),
+        )
+
+    multiply(0, even)
+
+    def step(k, carry):
+        n = 2 * k
+        multiply(n + 1, odd)
+        finish(n, even)
+        for store in stores(n):
+            store.start()
+        multiply(jnp.minimum(n + 2, CHUNKS - 1), even)
+        finish(n + 1, odd)
+        for store in stores(n + 1):
+            store.start()
+        return carry
+
+    lax.fori_loop(0, CHUNKS // 2, step, 0)
+
+    def drain(n, carry):
+        for store in stores(n):
+            store.wait()
+        return carry
+
+    lax.fori_loop(0, CHUNKS, drain, 0)
 
 
 def blend(spacing, faces, low, high, skel):
-    table, index = blend_tables()
-    whole = lambda *shape: pl.BlockSpec(shape, lambda q: (0,) * len(shape))
+    any_spec = pl.BlockSpec(memory_space=pl.ANY)
+    table = blend_table()
     return pl.pallas_call(
         blend_body,
         name="blend",
-        grid=(8,),
         out_shape=(
             jax.ShapeDtypeStruct((3, 8, 8, NP * NP), F32),
             jax.ShapeDtypeStruct((8, 8, NP * NP), F32),
         ),
-        in_specs=[
-            pl.BlockSpec(memory_space=pltpu.SMEM),
-            whole(3, 256, 128),
-            whole(3, 32, 128),
-            whole(3, 32, 128),
-            whole(8, 128),
-            whole(8, NP * NP),
-            whole(8, NP * NP),
+        in_specs=[pl.BlockSpec(memory_space=pltpu.SMEM)] + [any_spec] * 5,
+        out_specs=(any_spec, any_spec),
+        scratch_shapes=[
+            pltpu.VMEM(faces.shape, F32), pltpu.VMEM(low.shape, F32), pltpu.VMEM(high.shape, F32),
+            pltpu.VMEM(skel.shape, F32), pltpu.VMEM(table.shape, BF16),
+            pltpu.VMEM((2, 12 * LAYERS, 256), BF16), pltpu.VMEM((5, 6, 3, LAYERS, 128), F32),
+            pltpu.VMEM((12 * LAYERS, CHUNK), F32), pltpu.VMEM((12 * LAYERS, CHUNK), F32),
+            pltpu.VMEM((3, 8, 8, NP * NP), F32), pltpu.VMEM((8, 8, NP * NP), F32),
+            pltpu.SemaphoreType.DMA((5,)), pltpu.SemaphoreType.DMA((2, CHUNKS)),
         ],
-        out_specs=(
-            pl.BlockSpec((3, 1, 8, NP * NP), lambda q: (0, q, 0, 0)),
-            pl.BlockSpec((1, 8, NP * NP), lambda q: (q, 0, 0)),
-        ),
-        compiler_params=pltpu.CompilerParams(
-            dimension_semantics=("arbitrary",), vmem_limit_bytes=48 << 20
-        ),
-    )(spacing, faces, low, high, skel, jnp.asarray(table), jnp.asarray(index))
+        compiler_params=pltpu.CompilerParams(vmem_limit_bytes=63 << 20),
+    )(spacing, faces, low, high, skel, jnp.asarray(table))
 
 
 def on_device(disp, weight, owner, row, force, coupling, stiff, edges, spacing):

time: 86.4 us -> 70.7 us (0.82)
  local copies, waits for them, and re-layouts: 8.27 us -> 0 us
  Pallas kernels: 76.9 us -> 69.8 us
    unnamed x22 -> x0, local copies, waits for them, and re-layouts: 8.27 us -> none
    pallas_call x1, Pallas kernels: 62.6 us -> 58.1 us  [front(): pl.pallas_call(front_body, name='front', out_shape=(jax.ShapeDtypeStruct(...]
    pallas_call x1, Pallas kernels: 14.3 us -> 11.7 us  [blend(): pl.pallas_call(blend_body, name='blend', out_shape=(jax.ShapeDtypeStruct(...]
where the time goes in v3:
time: 70.7 us; the launch traced here: 70.6 us
  Pallas kernels  69.8 us (99%)
  between operations  0.8 us (1%)
    pallas_call x1, Pallas kernels, front(): pl.pallas_call(front_body, name='front', out_shape=(jax.ShapeDtypeStruct(...  58.1 us
    pallas_call x1, Pallas kernels, blend(): pl.pallas_call(blend_body, name='blend', out_shape=(jax.ShapeDtypeStruct(...  11.7 us

profile of v3, /device:TPU:1, one launch (start us, length us, event | category | flops | bytes accessed | tf_op | source)
XLA Modules:
  0.0 70.6 jit_solution(7122684737984479232)
XLA Ops:
  0.6 58.1 %front.1 = (f32[3,256,128]{2,1,0:T(8,128)}, f32[8,128]{1,0:T(8,128)}, f32[3,32,128]{2,1,0:T(8,128)}, f32[3,32,128]{2,1,0:T(8,128)}) custom-call(f32[3,2048]{1,0:T(4,128)} %disp_hbm.1, f32[4,2048]{1,0:T(4,128)} %bitcast.4, s32[4,2048]{1,0:T(4,128)} %bitcast.5, s32[4,2048]{1,0:T(4,128)} %bitcast.6, f32[3,64]{1,0:T(4,128)} %force_hbm.1, f32[6,64]{1,0:T(8,128)} %coupling_hbm.1, ...), custom_call_target="tpu_custom_call" | custom-call | tf_op jit(solution)/shard_map/front/pallas_call | solution.py:352
  58.7 11.7 %blend.1 = (f32[3,8,8,6400]{3,2,1,0:T(8,128)}, f32[8,8,6400]{2,1,0:T(8,128)}) custom-call(f32[3,8]{1,0:T(4,128)} %spacing_ref.1, f32[3,256,128]{2,1,0:T(8,128)} %get-tuple-element.6.faces_hbm, f32[3,32,128]{2,1,0:T(8,128)} %get-tuple-element.7.low_hbm, f32[3,32,128]{2,1,0:T(8,128)} %get-tuple-element.8.high_hbm, f32[8,128]{1,0:T(8,128)} %get-tuple-element.9.skel_hbm, ...), custom_call_target="tpu_custom_call" | custom-call | tf_op jit(solution)/shard_map/blend/pallas_call | solution.py:596

commit v4 on v3

--- a/solution.py
+++ b/solution.py
@@ -25,6 +25,100 @@
 def split(value):
     high = value.astype(BF16)
     return high, (value - high.astype(F32)).astype(BF16)
+
+
+CHUNK_J = 16
+CHUNK = CHUNK_J * NP
+CHUNKS = NP // CHUNK_J
+
+
+def blend_table():
+    f = np.arange(NP * NP)
+    i, j = f % NP, f // NP
+    n = NP - 1
+
+    def bubble(i, j):
+        s, t = i / n, j / n
+        return 16.0 * s * (1 - s) * t * (1 - t)
+
+    ip, im = np.minimum(i + 1, n), np.maximum(i - 1, 0)
+    jp, jm = np.minimum(j + 1, n), np.maximum(j - 1, 0)
+    hit = (j[None] % CHUNK_J == np.arange(CHUNK_J)[:, None]).astype(np.float64)
+    rows = [hit, hit * i, hit * (ip - im)]
+    for bump in (
+        bubble(i, j), 0.5 * (bubble(ip, j) - bubble(im, j)), 0.5 * (bubble(i, jp) - bubble(i, jm))
+    ):
+        high = bump.astype(BF16).astype(np.float64)
+        rows += [high[None], (bump - high)[None]]
+    rows.append(np.zeros((10, NP * NP)))
+    return np.concatenate(rows).astype(BF16)
+
+
+def column_of(values):
+    return jnp.concatenate([jnp.full((8, 128), value, F32) for value in values], axis=0)
+
+
+def two_parts(x, lane):
+    x = x + pltpu.roll(x, 64, axis=1)
+    high = x.astype(BF16).astype(F32)
+    return jnp.where(lane < 64, high, x - high).astype(BF16)
+
+
+def prepare(faces_ref, low_ref, high_ref, spacing_ref, lhs_ref, fns_ref):
+    span = lax.axis_index("span")
+    has_low = jnp.where(span > 0, 1.0, 0.0).astype(F32)
+    has_high = jnp.where(span < SPANS - 1, 1.0, 0.0).astype(F32)
+    lane = iota((LAYERS, 128), 1)
+    turn = iota((LAYERS, 128), 0) & 7
+    frac = lane.astype(F32) * (1.0 / (NP - 1))
+
+    def along_span(x, c, seg):
+        rows = [slice(seg * 8 + q, seg * 8 + q + 1) for q in range(8)]
+        before = jnp.concatenate([jnp.broadcast_to(low_ref[c, r, :], (8, 128)) for r in rows], axis=0)
+        after = jnp.concatenate([jnp.broadcast_to(high_ref[c, r, :], (8, 128)) for r in rows], axis=0)
+        nxt = jnp.where(turn == 7, after * has_high, pltpu.roll(x, LAYERS - 1, axis=0))
+        prv = jnp.where(turn == 0, before * has_low, pltpu.roll(x, 1, axis=0))
+        return 0.5 * (nxt - prv)
+
+    def along_lane(x):
+        nxt = jnp.where(lane == NP - 1, x, pltpu.roll(x, 127, axis=1))
+        prv = jnp.where(lane == 0, x, pltpu.roll(x, 1, axis=1))
+        return 0.5 * (nxt - prv)
+
+    def inner(x):
+        return x - (1.0 - frac) * x[:, 0:1] - frac * x[:, NP - 1 : NP]
+
+    for c in range(3):
+        now = [faces_ref[c, seg * LAYERS : (seg + 1) * LAYERS, :] for seg in range(4)]
+        diff = [along_span(x, c, seg) for seg, x in enumerate(now)]
+        values = []
+        for bottom, top, left, right in (now, diff):
+            base = inner(bottom)
+            values.append((base, inner(top) - base, left, (right - left) * (1.0 / (NP - 1))))
+        (b, d, left, m), (b_s, d_s, left_s, m_s) = values
+        b_i, left_j = along_lane(b), along_lane(left)
+        if c == 0:
+            b_i = b_i + column_of([spacing_ref[c, q] for q in range(8)])
+        elif c == 1:
+            left_j = left_j + column_of([spacing_ref[c, q] for q in range(8)])
+        else:
+            b_s = b_s + column_of([spacing_ref[c, q] for q in range(8)])
+        for n, fn in enumerate((b, d, b_i, along_lane(d), b_s, d_s)):
+            fns_ref[n, c] = fn
+        m_j = along_lane(m)
+        for chunk in range(CHUNKS):
+
+            def at(x, first):
+                shift = (first - chunk * CHUNK_J) % 128
+                return pltpu.roll(x, shift, axis=1) if shift else x
+
+            fields = [
+                jnp.where(lane < 16, at(x, 0), jnp.where(lane < 32, at(y, 16), 0.0))
+                for x, y in ((left, m), (left_j, m_j), (left_s, m_s))
+            ]
+            fields.insert(1, jnp.where((lane >= 32) & (lane < 48), at(0.5 * m, 32), 0.0))
+            for n, field in enumerate(fields):
+                lhs_ref[chunk, (n * 3 + c) * LAYERS : (n * 3 + c + 1) * LAYERS, :] = two_parts(field, lane)
 
 
 def wait_for(ref, sem):
@@ -110,12 +204,12 @@
 
 def front_body(
     disp_hbm, weight_hbm, owner_hbm, row_hbm, force_hbm, coupling_hbm, stiff_hbm, edges_hbm,
-    faces_ref, skel_ref, low_ref, high_ref,
+    spacing_hbm, lhs_hbm, fns_hbm, skel_ref,
     disp_ref, weight_ref, owner_ref, row_ref, force_ref, coupling_ref, stiff_ref, edges_ref,
-    lhs, rhs, send, recv, total,
+    spacing_ref, faces_ref, low_ref, high_ref, lhs_ref, fns_ref, lhs, rhs, send, recv, total,
     static, low_in, high_in, face_out, near, far, picks, weights, near_rows, far_rows, picks2, weights2,
     load_sem, send_sem, recv_sem, near_send, near_recv, far_send, far_recv, halo_send, halo_recv,
-    rows_send, rows_recv,
+    rows_send, rows_recv, result_sem,
 ):
     g, s = lax.axis_index("group"), lax.axis_index("span")
     up, down = (s + 1) % SPANS, (s + SPANS - 1) % SPANS
@@ -125,6 +219,7 @@
             [
                 (owner_hbm, owner_ref), (row_hbm, row_ref), (disp_hbm, disp_ref), (weight_hbm, weight_ref),
                 (coupling_hbm, coupling_ref), (stiff_hbm, stiff_ref), (edges_hbm, edges_ref), (force_hbm, force_ref),
+                (spacing_hbm, spacing_ref),
             ]
         )
     ]
@@ -144,20 +239,25 @@
     lax.fori_loop(1, SPANS, greet_span, 0)
     for load in loads:
         load.wait()
-    pack(disp_ref, weight_ref, owner_ref, row_ref, send, lhs, rhs)
-    recv[g] = send[g]
     diagonal = stiff_ref[...] + jnp.sum(coupling_ref[...], axis=0, keepdims=True)
+    share_rows, edge_rows = coupling_ref[...] / diagonal, edges_ref[...].astype(F32)
     blank = jnp.zeros((6, 64), F32)
-    static[0:6, :] = jnp.concatenate([coupling_ref[...] / diagonal, blank], axis=1)
-    static[8:14, :] = jnp.concatenate([edges_ref[...].astype(F32), blank], axis=1)
+    static[0:6, :] = jnp.concatenate([share_rows, blank], axis=1)
+    static[8:14, :] = jnp.concatenate([edge_rows, blank], axis=1)
     near_rows[g] = jnp.concatenate(
-        [
-            jnp.concatenate([coupling_ref[...] / diagonal, edges_ref[...].astype(F32)], axis=1),
-            jnp.zeros((2, 128), F32),
-        ],
-        axis=0,
+        [jnp.concatenate([share_rows, edge_rows], axis=1), jnp.zeros((2, 128), F32)], axis=0
     )
     pl.semaphore_wait(barrier, GROUPS - 1 + SPANS - 1)
+
+    def push_near_rows(k, carry):
+        pltpu.make_async_remote_copy(
+            near_rows.at[g], near_rows.at[g], rows_send.at[0], rows_recv.at[0],
+            device_id=(offset_peer(g, k), s), device_id_type=MESH,
+        ).start()
+        return carry
+
+    lax.fori_loop(0, GROUPS - 1, push_near_rows, 0)
+    pack(disp_ref, weight_ref, owner_ref, row_ref, send, lhs, rhs)
 
     def push_send(k, carry):
         peer = offset_peer(g, k)
@@ -167,6 +267,8 @@
         return carry
 
     lax.fori_loop(0, GROUPS - 1, push_send, 0)
+    own = pltpu.make_async_copy(send.at[g], recv.at[g], recv_sem.at[g])
+    own.start()
     halos = [
         pltpu.make_async_remote_copy(
             src, dst, halo_send.at[n], halo_recv.at[n], device_id=(g, to), device_id_type=MESH
@@ -180,16 +282,7 @@
     ]
     halos[0].start()
     halos[1].start()
-
-    def push_near_rows(k, carry):
-        pltpu.make_async_remote_copy(
-            near_rows.at[g], near_rows.at[g], rows_send.at[0], rows_recv.at[0],
-            device_id=(offset_peer(g, k), s), device_id_type=MESH,
-        ).start()
-        return carry
-
-    lax.fori_loop(0, GROUPS - 1, push_near_rows, 0)
-    total[...] = add_up(recv, [g])
+    total[...] = jnp.zeros_like(total)
     halos[0].wait_recv()
     halos[1].wait_recv()
     lane = iota((8, 128), 1)
@@ -236,12 +329,15 @@
         return carry
 
     lax.fori_loop(1, SPANS, push_far_rows, 0)
-    for k in range(0, GROUPS - 1, TOGETHER):
-        sources = [offset_peer(g, n) for n in range(k, min(k + TOGETHER, GROUPS - 1))]
+
+    def collect(m, carry):
+        sources = [offset_peer(g, m * TOGETHER + u) for u in range(TOGETHER)]
         for source in sources:
             wait_for(recv.at[source], recv_sem.at[source])
         total[...] += add_up(recv, sources)
-
+        return carry
+
+    lax.fori_loop(0, GROUPS // TOGETHER, collect, 0)
     row = iota((8, 128), 0)
     first = jnp.zeros((8, 128), F32)
     for c in range(3):
@@ -309,6 +405,10 @@
             out = jnp.where(row == c, functools.reduce(jnp.add, parts), out)
         return out
 
+    results = [
+        pltpu.make_async_copy(lhs_ref, lhs_hbm, result_sem.at[0]),
+        pltpu.make_async_copy(fns_ref, fns_hbm, result_sem.at[1]),
+    ]
     for r in range(ROUNDS):
         wait_for(near.at[r, pl.ds(0, GROUPS - 1)], near_recv.at[r])
         for h in range(16):
@@ -331,11 +431,16 @@
             sums = combine(table, picks2[...], weights2[...])
             near[1, g] = place(first + sums + pltpu.roll(sums, 64, axis=1))
             push_near(1)
+            halos[2].wait_recv()
+            halos[3].wait_recv()
+            prepare(faces_ref, low_ref, high_ref, spacing_ref, lhs_ref, fns_ref)
+            for copy in results:
+                copy.start()
         else:
             state = combine(table, picks[...], weights[...])
     skel_ref[...] = state
-    halos[2].wait_recv()
-    halos[3].wait_recv()
+    for copy in results:
+        copy.wait()
     wait_for(send.at[pl.ds(0, GROUPS - 1)], send_sem)
     for halo in halos:
         halo.wait_send()
@@ -346,22 +451,25 @@
         wait_for(far.at[r, pl.ds(0, SPANS - 1)], far_send.at[r])
 
 
-def front(disp, weight, owner, row, force, coupling, stiff, edges):
+def front(disp, weight, owner, row, force, coupling, stiff, edges, spacing):
     dma = pltpu.SemaphoreType.DMA
     local = [pltpu.VMEM(x.shape, x.dtype) for x in (disp, weight, owner, row, force, coupling, stiff, edges)]
+    any_spec = pl.BlockSpec(memory_space=pl.ANY)
+    lhs, fns = (CHUNKS, 12 * LAYERS, 128), (6, 3, LAYERS, 128)
     return pl.pallas_call(
         front_body,
         name="front",
         out_shape=(
-            jax.ShapeDtypeStruct((3, 256, 128), F32),
+            jax.ShapeDtypeStruct(lhs, BF16),
+            jax.ShapeDtypeStruct(fns, F32),
             jax.ShapeDtypeStruct((8, 128), F32),
-            jax.ShapeDtypeStruct((3, 32, 128), F32),
-            jax.ShapeDtypeStruct((3, 32, 128), F32),
         ),
-        in_specs=[pl.BlockSpec(memory_space=pltpu.HBM)] * 8,
-        out_specs=(VMEM_SPEC,) * 4,
+        in_specs=[any_spec] * 9,
+        out_specs=(any_spec, any_spec, VMEM_SPEC),
         scratch_shapes=[
-            *local,
+            *local, pltpu.SMEM(spacing.shape, F32),
+            pltpu.VMEM((3, 256, 128), F32), pltpu.VMEM((3, 32, 128), F32), pltpu.VMEM((3, 32, 128), F32),
+            pltpu.VMEM(lhs, BF16), pltpu.VMEM(fns, F32),
             pltpu.VMEM((512, NODES), BF16), pltpu.VMEM((256, NODES), BF16),
             pltpu.VMEM((GROUPS, 8, 256), F32), pltpu.VMEM((GROUPS, 8, 256), F32),
             pltpu.VMEM((6 * NP, 256), F32),
@@ -372,108 +480,14 @@
             pltpu.VMEM((128, 896), BF16), pltpu.VMEM((128, 896), F32),
             pltpu.VMEM((GROUPS, 8, 128), F32), pltpu.VMEM((SPANS, 192, 128), F32),
             pltpu.VMEM((128, 2304), BF16), pltpu.VMEM((128, 2304), F32),
-            dma((8,)), dma, dma((GROUPS,)),
+            dma((9,)), dma, dma((GROUPS,)),
             dma((ROUNDS,)), dma((ROUNDS,)), dma((ROUNDS,)), dma((ROUNDS,)), dma((4,)), dma((4,)),
-            dma((2,)), dma((2,)),
+            dma((2,)), dma((2,)), dma((2,)),
         ],
         compiler_params=pltpu.CompilerParams(
             collective_id=0, has_side_effects=True, vmem_limit_bytes=63 << 20
         ),
-    )(disp, weight, owner, row, force, coupling, stiff, edges)
-
-
-HALF = NP * NP // 2
-CHUNK = 640
-CHUNKS = NP * NP // CHUNK
-
-
-def blend_table():
-    f = np.arange(NP * NP)
-    i, j = f % NP, f // NP
-    n = NP - 1
-
-    def bubble(i, j):
-        s, t = i / n, j / n
-        return 16.0 * s * (1 - s) * t * (1 - t)
-
-    ip, im = np.minimum(i + 1, n), np.maximum(i - 1, 0)
-    jp, jm = np.minimum(j + 1, n), np.maximum(j - 1, 0)
-    hit = (j[None] % 40 == np.arange(40)[:, None]).astype(np.float64)
-    rows = [hit, hit * i, hit * (ip - im)]
-    for bump in (
-        bubble(i, j), 0.5 * (bubble(ip, j) - bubble(im, j)), 0.5 * (bubble(i, jp) - bubble(i, jm))
-    ):
-        high = bump.astype(BF16).astype(np.float64)
-        rows += [high[None], (bump - high)[None]]
-    rows.append(np.zeros((2, NP * NP)))
-    return np.concatenate(rows).astype(BF16)
-
-
-def column_of(values):
-    return jnp.concatenate([jnp.full((8, 128), value, F32) for value in values], axis=0)
-
-
-def prepare(faces_ref, low_ref, high_ref, spacing_ref, lhs_ref, fns_ref):
-    span = lax.axis_index("span")
-    has_low = jnp.where(span > 0, 1.0, 0.0).astype(F32)
-    has_high = jnp.where(span < SPANS - 1, 1.0, 0.0).astype(F32)
-    lane = iota((LAYERS, 128), 1)
-    turn = iota((LAYERS, 128), 0) & 7
-    frac = lane.astype(F32) * (1.0 / (NP - 1))
-
-    def along_span(x, c, seg):
-        rows = [slice(seg * 8 + q, seg * 8 + q + 1) for q in range(8)]
-        before = jnp.concatenate([jnp.broadcast_to(low_ref[c, r, :], (8, 128)) for r in rows], axis=0)
-        after = jnp.concatenate([jnp.broadcast_to(high_ref[c, r, :], (8, 128)) for r in rows], axis=0)
-        nxt = jnp.where(turn == 7, after * has_high, pltpu.roll(x, LAYERS - 1, axis=0))
-        prv = jnp.where(turn == 0, before * has_low, pltpu.roll(x, 1, axis=0))
-        return 0.5 * (nxt - prv)
-
-    def along_lane(x):
-        nxt = jnp.where(lane == NP - 1, x, pltpu.roll(x, 127, axis=1))
-        prv = jnp.where(lane == 0, x, pltpu.roll(x, 1, axis=1))
-        return 0.5 * (nxt - prv)
-
-    def inner(x):
-        return x - (1.0 - frac) * x[:, 0:1] - frac * x[:, NP - 1 : NP]
-
-    for c in range(3):
-        now = [faces_ref[c, seg * LAYERS : (seg + 1) * LAYERS, :] for seg in range(4)]
-        diff = [along_span(x, c, seg) for seg, x in enumerate(now)]
-        values = []
-        for bottom, top, left, right in (now, diff):
-            base = inner(bottom)
-            values.append((base, inner(top) - base, left, (right - left) * (1.0 / (NP - 1))))
-        (b, d, left, m), (b_s, d_s, left_s, m_s) = values
-        b_i, left_j = along_lane(b), along_lane(left)
-        if c == 0:
-            b_i = b_i + column_of([spacing_ref[c, q] for q in range(8)])
-        elif c == 1:
-            left_j = left_j + column_of([spacing_ref[c, q] for q in range(8)])
-        else:
-            b_s = b_s + column_of([spacing_ref[c, q] for q in range(8)])
-        for n, fn in enumerate((b, d, b_i, along_lane(d), b_s, d_s)):
-            for phase in range(5):
-                at = lane[0:8] + (phase * 128) % NP
-                at = jnp.where(at >= NP, at - NP, at)
-                at = jnp.where(at >= NP, at - NP, at)
-                for q in range(8):
-                    rows = slice(q * 8, q * 8 + 8)
-                    fns_ref[phase, n, c, rows, :] = jnp.take_along_axis(fn[rows], at, axis=1)
-        for half in range(2):
-            shift = (128 - 40 * half) % 128
-            fields = [None] * 4
-            for n, (x, y) in ((0, (left, m)), (2, (left_j, along_lane(m))), (3, (left_s, m_s))):
-                x = pltpu.roll(x, shift, axis=1) if half else x
-                y = y if half else pltpu.roll(y, 40, axis=1)
-                fields[n] = jnp.where(lane < 40, x, jnp.where(lane < 80, y, 0.0))
-            x = pltpu.roll(0.5 * m, 40 if half else 80, axis=1)
-            fields[1] = jnp.where((lane >= 80) & (lane < 120), x, 0.0)
-            for n, field in enumerate(fields):
-                high, low = split(field)
-                rows = slice((n * 3 + c) * LAYERS, (n * 3 + c + 1) * LAYERS)
-                lhs_ref[half, rows, 0:128] = high
-                lhs_ref[half, rows, 128:256] = low
+    )(disp, weight, owner, row, force, coupling, stiff, edges, spacing)
 
 
 def place_bumps(skel_ref, lhs_ref):
@@ -494,70 +508,69 @@
         nxt = jnp.where(turn[:, 0:1] == 7, nxt * has_high, nxt)
         prv = jnp.where(turn[:, 0:1] == 0, prv * has_low, prv)
         diff = 0.5 * (nxt - prv)
-        for n, (x, first) in enumerate(((value, 120), (value, 122), (value, 124), (diff, 120))):
+        for n, (x, first) in enumerate(((value, 48), (value, 50), (value, 52), (diff, 48))):
             rows = slice((n * 3 + c) * LAYERS, (n * 3 + c + 1) * LAYERS)
-            mine = (lane == first) | (lane == first + 1)
-            for part, cols in zip(split(jnp.where(mine, x, 0.0)), (slice(0, 128), slice(128, 256))):
-                for half in range(2):
-                    lhs_ref[half, rows, cols] = lhs_ref[half, rows, cols] + part
+            mine = (lane & 63 == first) | (lane & 63 == first + 1)
+            high = x.astype(BF16).astype(F32)
+            bump = jnp.where(mine, jnp.where(lane < 64, high, x - high), 0.0).astype(BF16)
+            for chunk in range(CHUNKS):
+                lhs_ref[chunk, rows, :] = lhs_ref[chunk, rows, :] + bump
 
 
 def blend_body(
-    spacing_ref, faces_hbm, low_hbm, high_hbm, skel_hbm, table_hbm, disp_hbm, jac_hbm,
-    faces_ref, low_ref, high_ref, skel_ref, table_ref, lhs_ref, fns_ref, even, odd, disp_ref, jac_ref,
-    load_sem, store_sem,
+    lhs_hbm, fns_hbm, skel_hbm, table_hbm, disp_hbm, jac_hbm,
+    lhs_ref, fns_ref, skel_ref, table_ref, picked, even, odd, disp_ref, jac_ref, load_sem, store_sem,
 ):
     loads = [
         pltpu.make_async_copy(src, dst, load_sem.at[n])
         for n, (src, dst) in enumerate(
-            [
-                (faces_hbm, faces_ref), (low_hbm, low_ref), (high_hbm, high_ref), (skel_hbm, skel_ref),
-                (table_hbm, table_ref),
-            ]
+            [(skel_hbm, skel_ref), (lhs_hbm, lhs_ref), (table_hbm, table_ref), (fns_hbm, fns_ref)]
         )
     ]
     for load in loads:
         load.start()
-    for load in loads[:4]:
-        load.wait()
-    prepare(faces_ref, low_ref, high_ref, spacing_ref, lhs_ref, fns_ref)
+    loads[0].wait()
+    loads[1].wait()
     place_bumps(skel_ref, lhs_ref)
-    loads[4].wait()
+    loads[2].wait()
+    loads[3].wait()
 
     def cols_of(n):
         return pl.ds(pl.multiple_of(n * CHUNK, 128), CHUNK)
 
     def multiply(n, out):
         table = table_ref[:, cols_of(n)]
-        out[...] = jnp.dot(
-            lhs_ref[n // (CHUNKS // 2)], jnp.concatenate([table, table], axis=0), preferred_element_type=F32
-        )
+        out[...] = jnp.dot(lhs_ref[n], jnp.concatenate([table, table], axis=0), preferred_element_type=F32)
 
     def finish(n, found):
         place = iota((8, 128), 1)
         for phase in range(5):
-            cols = slice(phase * 128, (phase + 1) * 128)
-            far = place + phase * 128
-            j = n * (CHUNK // NP) + sum(jnp.where(far >= NP * k, 1, 0) for k in range(1, CHUNK // NP))
-            t = j.astype(F32) * (1.0 / (NP - 1))
-            t_j = jnp.where((j == 0) | (j == NP - 1), 0.5 / (NP - 1), 1.0 / (NP - 1))
-            out_cols = pl.ds(pl.multiple_of(n * CHUNK + phase * 128, 128), 128)
+            turns = []
+            for turn in range(2):
+                far = place + phase * 128
+                j = n * CHUNK_J + turn * 8 + sum(jnp.where(far >= NP * k, 1, 0) for k in range(1, 8))
+                t = j.astype(F32) * (1.0 / (NP - 1))
+                t_j = jnp.where((j == 0) | (j == NP - 1), 0.5 / (NP - 1), 1.0 / (NP - 1))
+                first = turn * 640 + phase * 128
+                out_cols = pl.ds(pl.multiple_of(n * CHUNK + first, 128), 128)
+                turns.append((t, t_j, slice(first, first + 128), out_cols))
             for q in range(8):
-                matrix = []
-                for c in range(3):
-                    b, d, b_i, d_i, b_s, d_s = [
-                        fns_ref[phase, k, c, q * 8 : q * 8 + 8, :] for k in range(6)
-                    ]
-                    x, x_i, x_j, x_s = [
-                        found[(k * 3 + c) * LAYERS + q * 8 : (k * 3 + c) * LAYERS + q * 8 + 8, cols]
-                        for k in range(4)
-                    ]
-                    disp_ref[c, q, :, out_cols] = x + b + t * d
-                    matrix.append([x_i + b_i + t * d_i, x_j + t_j * d, x_s + b_s + t * d_s])
-                one = matrix[1][1] * matrix[2][2] - matrix[1][2] * matrix[2][1]
-                two = matrix[1][0] * matrix[2][2] - matrix[1][2] * matrix[2][0]
-                three = matrix[1][0] * matrix[2][1] - matrix[1][1] * matrix[2][0]
-                jac_ref[q, :, out_cols] = matrix[0][0] * one - matrix[0][1] * two + matrix[0][2] * three
+                lines = slice(q * 8, q * 8 + 8)
+                fns = [[picked[phase, k, c, lines, :] for k in range(6)] for c in range(3)]
+                for t, t_j, cols, out_cols in turns:
+                    matrix = []
+                    for c in range(3):
+                        b, d, b_i, d_i, b_s, d_s = fns[c]
+                        x, x_i, x_j, x_s = [
+                            found[(k * 3 + c) * LAYERS + q * 8 : (k * 3 + c) * LAYERS + q * 8 + 8, cols]
+                            for k in range(4)
+                        ]
+                        disp_ref[c, q, :, out_cols] = x + b + t * d
+                        matrix.append([x_i + b_i + t * d_i, x_j + t_j * d, x_s + b_s + t * d_s])
+                    one = matrix[1][1] * matrix[2][2] - matrix[1][2] * matrix[2][1]
+                    two = matrix[1][0] * matrix[2][2] - matrix[1][2] * matrix[2][0]
+                    three = matrix[1][0] * matrix[2][1] - matrix[1][1] * matrix[2][0]
+                    jac_ref[q, :, out_cols] = matrix[0][0] * one - matrix[0][1] * two + matrix[0][2] * three
 
     def stores(n):
         cols = cols_of(n)
@@ -566,21 +579,35 @@
             pltpu.make_async_copy(jac_ref.at[:, :, cols], jac_hbm.at[:, :, cols], store_sem.at[1, n]),
         )
 
+    def start(n):
+        for store in stores(n):
+            store.start()
+
     multiply(0, even)
+    lane = iota((8, 128), 1)
+    for phase in range(5):
+        at = lane + (phase * 128) % NP
+        at = jnp.where(at >= NP, at - NP, at)
+        at = jnp.where(at >= NP, at - NP, at)
+        for n in range(6):
+            for c in range(3):
+                for q in range(8):
+                    lines = slice(q * 8, q * 8 + 8)
+                    picked[phase, n, c, lines, :] = jnp.take_along_axis(fns_ref[n, c, lines, :], at, axis=1)
 
     def step(k, carry):
         n = 2 * k
         multiply(n + 1, odd)
         finish(n, even)
-        for store in stores(n):
-            store.start()
-        multiply(jnp.minimum(n + 2, CHUNKS - 1), even)
+        start(n)
+        multiply(n + 2, even)
         finish(n + 1, odd)
-        for store in stores(n + 1):
-            store.start()
+        start(n + 1)
         return carry
 
     lax.fori_loop(0, CHUNKS // 2, step, 0)
+    finish(CHUNKS - 1, even)
+    start(CHUNKS - 1)
 
     def drain(n, carry):
         for store in stores(n):
@@ -590,7 +617,7 @@
     lax.fori_loop(0, CHUNKS, drain, 0)
 
 
-def blend(spacing, faces, low, high, skel):
+def blend(lhs, fns, skel):
     any_spec = pl.BlockSpec(memory_space=pl.ANY)
     table = blend_table()
     return pl.pallas_call(
@@ -600,25 +627,24 @@
             jax.ShapeDtypeStruct((3, 8, 8, NP * NP), F32),
             jax.ShapeDtypeStruct((8, 8, NP * NP), F32),
         ),
-        in_specs=[pl.BlockSpec(memory_space=pltpu.SMEM)] + [any_spec] * 5,
+        in_specs=[any_spec] * 4,
         out_specs=(any_spec, any_spec),
         scratch_shapes=[
-            pltpu.VMEM(faces.shape, F32), pltpu.VMEM(low.shape, F32), pltpu.VMEM(high.shape, F32),
-            pltpu.VMEM(skel.shape, F32), pltpu.VMEM(table.shape, BF16),
-            pltpu.VMEM((2, 12 * LAYERS, 256), BF16), pltpu.VMEM((5, 6, 3, LAYERS, 128), F32),
+            pltpu.VMEM(lhs.shape, BF16), pltpu.VMEM(fns.shape, F32), pltpu.VMEM(skel.shape, F32),
+            pltpu.VMEM(table.shape, BF16), pltpu.VMEM((5, 6, 3, LAYERS, 128), F32),
             pltpu.VMEM((12 * LAYERS, CHUNK), F32), pltpu.VMEM((12 * LAYERS, CHUNK), F32),
             pltpu.VMEM((3, 8, 8, NP * NP), F32), pltpu.VMEM((8, 8, NP * NP), F32),
-            pltpu.SemaphoreType.DMA((5,)), pltpu.SemaphoreType.DMA((2, CHUNKS)),
+            pltpu.SemaphoreType.DMA((4,)), pltpu.SemaphoreType.DMA((2, CHUNKS)),
         ],
         compiler_params=pltpu.CompilerParams(vmem_limit_bytes=63 << 20),
-    )(spacing, faces, low, high, skel, jnp.asarray(table))
+    )(lhs, fns, skel, jnp.asarray(table))
 
 
 def on_device(disp, weight, owner, row, force, coupling, stiff, edges, spacing):
-    faces, skel, low, high = front(
-        disp, weight.T, owner.T, row.T, force, coupling, stiff.reshape(1, -1), edges
+    lhs, fns, skel = front(
+        disp, weight.T, owner.T, row.T, force, coupling, stiff.reshape(1, -1), edges, spacing
     )
-    return blend(spacing, faces, low, high, skel)
+    return blend(lhs, fns, skel)
 
 
 def solution(mesh):

time: 70.7 us -> 60 us (0.85)
  Pallas kernels: 69.8 us -> 59.2 us
    pallas_call x1, Pallas kernels: 58.1 us -> 51.6 us  [front(): pl.pallas_call(front_body, name='front', out_shape=(jax.ShapeDtypeStruct(...]
    pallas_call x1, Pallas kernels: 11.7 us -> 7.64 us  [blend(): pl.pallas_call(blend_body, name='blend', out_shape=(jax.ShapeDtypeStruct(...]
where the time goes in v4:
time: 60 us; the launch traced here: 59.8 us
  Pallas kernels  59.2 us (99%)
  between operations  0.64 us (1%)
    pallas_call x1, Pallas kernels, front(): pl.pallas_call(front_body, name='front', out_shape=(jax.ShapeDtypeStruct(...  51.6 us
    pallas_call x1, Pallas kernels, blend(): pl.pallas_call(blend_body, name='blend', out_shape=(jax.ShapeDtypeStruct(...  7.64 us

profile of v4, /device:TPU:1, one launch (start us, length us, event | category | flops | bytes accessed | tf_op | source)
XLA Modules:
  0.0 59.8 jit_solution(2569820257980822076)
XLA Ops:
  0.6 51.6 %front.1 = (bf16[5,768,128]{2,1,0:T(8,128)(2,1)}, f32[6,3,64,128]{3,2,1,0:T(8,128)}, f32[8,128]{1,0:T(8,128)}) custom-call(f32[3,2048]{1,0:T(4,128)} %disp_hbm.1, f32[4,2048]{1,0:T(4,128)} %bitcast.4, s32[4,2048]{1,0:T(4,128)} %bitcast.5, s32[4,2048]{1,0:T(4,128)} %bitcast.6, f32[3,64]{1,0:T(4,128)} %force_hbm.1, f32[6,64]{1,0:T(8,128)} %coupling_hbm.1, ...), custom_call_target="tpu_custom_call" | custom-call | tf_op jit(solution)/shard_map/front/pallas_call | solution.py:459
  52.2 7.6 %blend.1 = (f32[3,8,8,6400]{3,2,1,0:T(8,128)}, f32[8,8,6400]{2,1,0:T(8,128)}) custom-call(bf16[5,768,128]{2,1,0:T(8,128)(2,1)} %get-tuple-element.5.lhs_hbm, f32[6,3,64,128]{3,2,1,0:T(8,128)} %get-tuple-element.6.fns_hbm, f32[8,128]{1,0:T(8,128)} %get-tuple-element.7.skel_hbm, bf16[64,6400]{1,0:T(8,128)(2,1)} %constant.2.clone.table_hbm), custom_call_target="tpu_custom_call" | custom-call | tf_op jit(solution)/shard_map/blend/pallas_call | solution.py:623

commit v5 on v4

--- a/solution.py
+++ b/solution.py
@@ -148,20 +148,21 @@
         base += jnp.dot(piece, every, preferred_element_type=F32)
     rank = jnp.concatenate(ranks, axis=1)
     word = iota((8, NODES), 0) & 3
-    total = jnp.zeros((512, 256), F32)
-    for t in range(4):
-        owner = owner_ref[t : t + 1, :]
+
+    def one(t, total):
+        line_t = pl.ds(t, 1)
+        owner = owner_ref[line_t, :]
         slot = jnp.sum(jnp.where(owner == group_rows, rank, 0.0), axis=0, keepdims=True).astype(I32)
         half = slot >> 8
         column = slot & 255
         bucket = owner * 2 + half
-        row = row_ref[t : t + 1, :]
+        row = row_ref[line_t, :]
         layer = ((row >> 6) * 205) >> 10
         edge = row - layer * (4 * NP)
         seg = ((edge >> 4) * 205) >> 10
         along = (edge - seg * NP) << 8
         line = seg * LAYERS + layer
-        weight = weight_ref[t : t + 1, :]
+        weight = weight_ref[line_t, :]
         value = jnp.where(
             word == 0, disp_ref[0:1, :], jnp.where(word == 1, disp_ref[1:2, :], disp_ref[2:3, :])
         ) * weight
@@ -174,7 +175,9 @@
         lhs[0:256, :] = jnp.where(hit, high, zero)
         lhs[256:512, :] = jnp.where(hit, low, zero)
         rhs[...] = jnp.where(iota((256, NODES), 0) == column, 1.0, 0.0).astype(BF16)
-        total += lax.dot_general(lhs[...], rhs[...], NT, preferred_element_type=F32)
+        return total + lax.dot_general(lhs[...], rhs[...], NT, preferred_element_type=F32)
+
+    total = lax.fori_loop(0, 4, one, jnp.zeros((512, 256), F32))
     out_ref[...] = (total[0:256] + total[256:512]).reshape(GROUPS, 8, 256)
 
 

time: 60 us -> 60.5 us (level)
  no operation moved by 1% of the time
where the time goes in v5:
time: 60.5 us; the launch traced here: 60.4 us
  Pallas kernels  59.7 us (99%)
  between operations  0.64 us (1%)
    pallas_call x1, Pallas kernels, front(): pl.pallas_call(front_body, name='front', out_shape=(jax.ShapeDtypeStruct(...  52.1 us
    pallas_call x1, Pallas kernels, blend(): pl.pallas_call(blend_body, name='blend', out_shape=(jax.ShapeDtypeStruct(...  7.64 us

profile of v5, /device:TPU:1, one launch (start us, length us, event | category | flops | bytes accessed | tf_op | source)
XLA Modules:
  0.0 60.4 jit_solution(5689331226327173047)
XLA Ops:
  0.6 52.1 %front.1 = (bf16[5,768,128]{2,1,0:T(8,128)(2,1)}, f32[6,3,64,128]{3,2,1,0:T(8,128)}, f32[8,128]{1,0:T(8,128)}) custom-call(f32[3,2048]{1,0:T(4,128)} %disp_hbm.1, f32[4,2048]{1,0:T(4,128)} %bitcast.4, s32[4,2048]{1,0:T(4,128)} %bitcast.5, s32[4,2048]{1,0:T(4,128)} %bitcast.6, f32[3,64]{1,0:T(4,128)} %force_hbm.1, f32[6,64]{1,0:T(8,128)} %coupling_hbm.1, ...), custom_call_target="tpu_custom_call" | custom-call | tf_op jit(solution)/shard_map/front/pallas_call | solution.py:462
  52.7 7.6 %blend.1 = (f32[3,8,8,6400]{3,2,1,0:T(8,128)}, f32[8,8,6400]{2,1,0:T(8,128)}) custom-call(bf16[5,768,128]{2,1,0:T(8,128)(2,1)} %get-tuple-element.5.lhs_hbm, f32[6,3,64,128]{3,2,1,0:T(8,128)} %get-tuple-element.6.fns_hbm, f32[8,128]{1,0:T(8,128)} %get-tuple-element.7.skel_hbm, bf16[64,6400]{1,0:T(8,128)(2,1)} %constant.2.clone.table_hbm), custom_call_target="tpu_custom_call" | custom-call | tf_op jit(solution)/shard_map/blend/pallas_call | solution.py:626
